TPU v7x, 256 devices: a whole 4x4x8 slice. The times are simulated.
256 devices in a mesh: row: 8 (over x, y_hi), grp: 32 (over z, y_lo, core).
Axes of the slice: x: 4, y: 4 (y_hi: 2, y_lo: 2; y = y_hi * 2 + y_lo), z: 8, core: 2. Of those that a mesh axis runs over, the one named last changes fastest.
Arguments:
- segments: bfloat16 [32, 128, 128, 512], P('grp', 'row'), may hold values from -40 to 40
- conv_weight: bfloat16 [3, 512, 512], replicated, may hold values from -0.15625 to 0.15625
- gain: float32 [512], replicated, may hold values from 0.1 to 1.9
- head: bfloat16 [512, 128], replicated, may hold values from -0.25 to 0.25
- group: int32 [32, 128], P('grp', 'row'), may hold values from 0 to 7
- positive: int32 [32, 128], P('grp', 'row'), may hold values from 0 to 127, as said below
Outputs:
- grad_conv: float32 [3, 512, 512], replicated
- grad_gain: float32 [512], replicated
- projector_derivative: float32 [512, 128], replicated
Inputs may be any that keep to these rules, and one draw needn't show every extreme that they name: positive[c, i] is another segment of the same index c with the same group, and positive[c, positive[c, i]] == i.
All inputs are finite; a program needn't handle non-finite values.
Results may differ from a plain program's by a relative error of at most 0.003.
The roundings to bfloat16 on the way count: a program that leaves them out, or rounds other values in their place, can miss the bound.
Values sent between devices are 32-bit elements; how exact they have to be, the bound alone decides.
No kernel may reach another device: no remote copies, remote signals or barrier semaphores. Data moves between devices by JAX's collectives and lax.ppermute only.
A program may use at most 64 MiB of HBM per device.

v0:
```python
from functools import partial

import jax
import jax.numpy as jnp
from jax import lax
from jax.sharding import PartitionSpec as P

DILATION_GAP = 2


logit_divisor = 0.1


def unit_rows(values):
    return values * lax.rsqrt(jnp.mean(values * values, axis=-1, keepdims=True) + 1e-05)


def scale_embed(projected):
    return unit_rows(projected) * projected.shape[-1] ** (-0.5)


def filter_tap_window(normalized_rows, filter_tap_index, spacing):
    sequence_length = normalized_rows.shape[1]
    padded = jnp.pad(normalized_rows, ((0, 0), (spacing, spacing), (0, 0)))
    return padded[:, filter_tap_index * spacing : filter_tap_index * spacing + sequence_length]


def reverse_tap_gather(term, filter_tap_index, spacing):
    sequence_length = term.shape[1]
    padded = jnp.pad(term, ((0, 0), (spacing, spacing), (0, 0)))
    begin = (2 - filter_tap_index) * spacing
    return padded[:, begin : begin + sequence_length]


def encode(patient_piece_records, conv_weight, gain, head):
    inputs = patient_piece_records.astype(jnp.float32)
    unit = unit_rows(inputs)
    normalized_rows = (unit * gain).astype(jnp.bfloat16)
    segment_count, sequence_length, channel_count = normalized_rows.shape
    conv = jnp.zeros((segment_count * sequence_length, channel_count), jnp.float32)
    for filter_tap_index in range(conv_weight.shape[0]):
        shifted_input = filter_tap_window(normalized_rows, filter_tap_index, DILATION_GAP).reshape(
            segment_count * sequence_length, channel_count
        )
        conv = conv + jnp.dot(
            shifted_input, conv_weight[filter_tap_index], preferred_element_type=jnp.float32
        )
    conv = conv.reshape(segment_count, sequence_length, channel_count)
    hidden = inputs + jax.nn.gelu(conv, approximate=True)
    pooled = jnp.mean(hidden, axis=1).astype(jnp.bfloat16)
    projected = jnp.dot(pooled, head, preferred_element_type=jnp.float32)
    return (unit, normalized_rows, conv, pooled, projected)


def backward(embed_grad, unit, normalized_rows, conv, pooled, projected, conv_weight, head):
    projected_grad = jax.vjp(scale_embed, projected)[1](embed_grad)[0]
    projector_derivative = jnp.dot(
        pooled.astype(jnp.float32).T, projected_grad, precision=lax.Precision.HIGHEST
    )
    pooled_grad = jnp.dot(
        projected_grad, head.astype(jnp.float32).T, precision=lax.Precision.HIGHEST
    )
    segment_count, sequence_length, channel_count = conv.shape
    hidden_grad = jnp.broadcast_to(pooled_grad[:, None, :] / sequence_length, conv.shape)
    conv_grad = jax.vjp(partial(jax.nn.gelu, approximate=True), conv)[1](hidden_grad)[0].astype(
        jnp.bfloat16
    )
    flat_grad = conv_grad.reshape(segment_count * sequence_length, channel_count)
    tap_grads = []
    normalized_gradient = jnp.zeros((segment_count, sequence_length, channel_count), jnp.float32)
    for filter_tap_index in range(conv_weight.shape[0]):
        shifted_input = filter_tap_window(normalized_rows, filter_tap_index, DILATION_GAP).reshape(
            segment_count * sequence_length, channel_count
        )
        tap_grads.append(
            lax.dot_general(
                shifted_input,
                flat_grad,
                (((0,), (0,)), ((), ())),
                preferred_element_type=jnp.float32,
            )
        )
        backward_term = lax.dot_general(
            flat_grad,
            conv_weight[filter_tap_index],
            (((1,), (1,)), ((), ())),
            preferred_element_type=jnp.float32,
        )
        normalized_gradient = normalized_gradient + reverse_tap_gather(
            backward_term.reshape(segment_count, sequence_length, channel_count),
            filter_tap_index,
            DILATION_GAP,
        )
    grad_conv = jnp.stack(tap_grads)
    grad_gain = jnp.sum(normalized_gradient * unit, axis=(0, 1))
    return (grad_conv, grad_gain, projector_derivative)


def body(segments, conv_weight, gain, head, group, positive):
    patient_piece_records = segments[0]
    group_ids = group[0]
    partners = positive[0]
    unit, normalized_rows, conv, pooled, projected = encode(
        patient_piece_records, conv_weight, gain, head
    )
    encounter_latent_vector = scale_embed(projected)
    gathered_embedding, all_groups = (
        lax.all_gather(encounter_latent_vector, "row", axis=0, tiled=True),
        lax.all_gather(group_ids, "row", axis=0, tiled=True),
    )
    local_count = encounter_latent_vector.shape[0]
    matrix_height_number = gathered_embedding.shape[0]
    global_multiplier = (matrix_height_number * lax.axis_size("grp")) ** (-0.5) / logit_divisor
    own_rows = lax.axis_index("row") * local_count + jnp.arange(local_count, dtype=jnp.int32)
    columns = jnp.arange(matrix_height_number, dtype=jnp.int32)
    cosine_affinity_matrix = (
        jnp.dot(encounter_latent_vector, gathered_embedding.T, precision=lax.Precision.HIGHEST)
        / logit_divisor
    )
    same_group = (group_ids[:, None] == all_groups[None, :]) & (
        own_rows[:, None] != columns[None, :]
    )
    log_total = jnp.log(
        jnp.sum(jnp.where(same_group, jnp.exp(cosine_affinity_matrix), 0.0), axis=1)
    )
    softmax = jnp.where(same_group, jnp.exp(cosine_affinity_matrix - log_total[:, None]), 0.0)
    row_term = jnp.dot(softmax, gathered_embedding, precision=lax.Precision.HIGHEST)
    partner_pick = (partners[:, None] == columns[None, :]).astype(jnp.float32)
    partner_embed = jnp.dot(partner_pick, gathered_embedding, precision=lax.Precision.HIGHEST)
    column_term = lax.psum_scatter(
        lax.dot_general(
            softmax,
            encounter_latent_vector,
            (((0,), (0,)), ((), ())),
            precision=lax.Precision.HIGHEST,
            preferred_element_type=jnp.float32,
        ),
        "row",
        scatter_dimension=0,
        tiled=True,
    )
    embed_grad = global_multiplier * (row_term + column_term - 2.0 * partner_embed)
    grads = backward(embed_grad, unit, normalized_rows, conv, pooled, projected, conv_weight, head)
    grads = lax.psum((grads[0], grads[1], grads[2]), ("row", "grp"))
    return (grads[0], grads[1], grads[2])


def solution(mesh):
    placed = (P("grp", "row", None, None), P(), P(), P(), P("grp", "row"), P("grp", "row"))
    return jax.shard_map(
        body, mesh=mesh, in_specs=placed, out_specs=(P(), P(), P()), check_vma=False
    )
```

profile of v0, /device:TPU:1, one launch (start us, length us, event | category | flops | bytes accessed | tf_op | source)
XLA Modules:
  0.0 476.3 jit_solution(5161826225677553854)
XLA Ops:
  7.2 0.0 copy-start
  7.2 0.0 copy-start.10
  7.2 0.0 reduce-scatter.2.cloned.1.call-start
  7.2 3.0 copy.23
  10.3 0.4 fusion.7
  10.7 0.0 copy-done.10
  10.7 0.7 fusion.5
  11.4 0.0 copy-start.5
  11.4 2.1 fusion.10
  13.5 3.2 pad_slice_fusion.2
  16.7 0.0 copy-done.5
  16.7 3.9 copy.24
  20.6 3.9 copy.25
  24.6 5.0 %fusion.45 = f32[2048,512]{1,0:T(8,128)} fusion(bf16[2048,512]{1,0:T(8,128)(2,1)} %bitcast.96, bf16[3,512,512]{2,1,0:T(8,128)(2,1)} %param.7), kind=kOutput, calls=%fused_computation.63 | convolution fusion | flops 1073741824 | bytes 6815744 | tf_op jit(solution)/shard_map/dot_general | solution.py:45
  29.6 0.0 copy-done.4
  29.6 4.3 fusion.43
  33.9 3.9 copy.26
  37.8 7.4 %add_add_fusion = f32[2048,512]{1,0:T(8,128)} fusion(f32[2048,512]{1,0:T(8,128)} %fusion.45, f32[2048,512]{1,0:T(8,128)} %fusion.43, bf16[2048,512]{1,0:T(8,128)(2,1)} %bitcast.98, bf16[3,512,512]{2,1,0:T(8,128)(2,1)} %param.7), kind=kOutput, calls=%fused_computation.44 | convolution fusion | flops 1075838976 | bytes 15204352 | tf_op jit(solution)/shard_map/dot_general | solution.py:45
  45.2 5.3 %copy.30 = f32[16,128,512]{1,2,0:T(8,128)} copy(f32[16,128,512]{2,1,0:T(8,128)} %bitcast.91) | data formatting | bytes 8388608 | tf_op jit(solution)/shard_map/reshape | solution.py:48
  50.5 3.4 fusion.8
  53.9 0.0 copy-done
  54.0 0.2 multiply_reduce_fusion.1
  54.2 0.0 copy-done.13
  54.2 0.6 dynamic-slice
  55.5 0.0 copy-done.12
  55.5 0.1 bitcast_dynamic-update-slice_fusion
  55.6 11.1 %all-reduce.3 = s32[128]{0:T(128)S(1)} all-reduce(s32[128]{0:T(128)S(1)} %bitcast_dynamic-update-slice_fusion), channel_id=2, replica_groups=mesh['row'=8,'grp'=32] {'row'}, use_global_device_ids=true, to_apply=%add.3 | all-reduce | flops 128 | bytes 1024
  66.7 0.1 multiply_multiply_fusion.4
  66.8 27.9 %all_gather.7 = f32[128,128]{1,0:T(8,128)S(1)} all-gather(f32[16,128]{1,0:T(8,128)S(1)} %multiply_multiply_fusion.4), channel_id=1, replica_groups=mesh['row'=8,'grp'=32] {'row'}, dimensions={0}, use_global_device_ids=true | all-gather | bytes 73728 | tf_op jit(solution)/shard_map/all_gather | solution.py:108
  94.7 0.3 select_reduce_fusion
  95.0 1.0 fusion.56
  96.0 0.0 reduce-scatter.2.cloned.1.call-update
  96.1 0.2 all-reduce.7.cloned.1.call-start
  96.3 83.6 %reduce-scatter.2.cloned.1.call-done = f32[16,128]{1,0:T(8,128)} async-done(((f32[128,128]{1,0:T(8,128)}), f32[16,128]{1,0:T(8,128)}) %reduce-scatter.2.cloned.1.call-update) | async-done | bytes 8208 | tf_op jit(solution)/shard_map/reduce_scatter | solution.py:130
  179.9 1.1 convolution_add_fusion
  181.0 0.0 copy-done.11
  181.0 0.3 multiply_reduce_fusion
  181.3 0.3 broadcast_multiply_fusion
  181.6 6.5 %fusion.17 = bf16[16,128,512]{1,2,0:T(8,128)(2,1)S(1)} fusion(f32[16,128,512]{1,2,0:T(8,128)} %copy.30, f32[16,512]{1,0:T(8,128)S(1)} %get-tuple-element.8, f32[16,512]{1,0:T(8,128)S(1)} %get-tuple-element.7), kind=kLoop, calls=%fused_computation.27 | loop fusion | flops 19922944 | bytes 6356992 | tf_op jit(solution)/shard_map/convert_element_type | solution.py:65
  188.0 0.0 copy-done.1
  188.0 0.0 copy-start.6
  188.0 2.7 fusion.24
  190.7 0.0 copy-done.6
  190.8 0.0 copy-start.2
  190.8 1.3 convolution_bitcast_fusion
  192.1 0.0 copy-start.7
  192.1 1.3 convolution_bitcast_fusion.1
  193.4 1.0 fusion.54
  194.4 0.0 copy-done.2
  194.4 0.0 copy-done.7
  194.4 1.2 fusion.33
  195.7 2.0 pad_maximum_fusion
  197.6 0.0 all-reduce.7.cloned.1.call-update
  197.7 0.0 copy-start.3
  197.7 0.0 copy-start.8
  197.7 3.1 fusion.40
  200.8 0.0 copy-done.3
  200.8 0.0 copy-done.8
  200.8 1.3 fusion.37
  202.1 2.6 fusion.6
  204.7 77.7 %psum.22 = f32[512]{0:T(512)} all-reduce(f32[512]{0:T(512)S(1)} %fusion.6), channel_id=1, replica_groups=mesh['row'=8,'grp'=32] {'row','grp'}, use_global_device_ids=true, to_apply=%region_8.9 | all-reduce | flops 512 | bytes 4096 | tf_op jit(solution)/shard_map/psum | solution.py:144
  282.4 182.4 %all-reduce.7.cloned.1.call-done = (f32[3,512,512]{2,1,0:T(8,128)}, f32[512,128]{1,0:T(8,128)}) async-done(((f32[3,512,512]{2,1,0:T(8,128)}, f32[512,128]{1,0:T(8,128)}), (f32[3,512,512]{2,1,0:T(8,128)}, f32[512,128]{1,0:T(8,128)})) %all-reduce.7.cloned.1.call-update) | async-done | bytes 3407888 | tf_op jit(solution)/shard_map/psum | solution.py:144
  464.9 3.9 copy.50
  468.8 0.7 copy.51
  (13 shorter events, 0.0 us)
Async XLA Ops:
  7.2 46.8 %copy-start = (bf16[512,128]{1,0:T(8,128)(2,1)S(1)}, bf16[512,128]{1,0:T(8,128)(2,1)}, u32[]{:S(2)}) copy-start(bf16[512,128]{1,0:T(8,128)(2,1)} %param.9) | copy-start | bytes 393220
  7.2 3.5 copy-start.10
  7.2 172.7 %reduce-scatter.2.cloned.1.call-start = ((), (), s32[]{:S(2)}) async-start(), calls=%async_computation.1 | async-start | bytes 73728 | tf_op jit(solution)/shard_map/reduce_scatter | solution.py:130
  11.4 5.3 %copy-start.5 = (bf16[16,128,512]{1,2,0:T(8,128)(2,1)}, bf16[16,128,512]{1,2,0:T(8,128)(2,1)S(1)}, u32[]{:S(2)}) copy-start(bf16[16,128,512]{1,2,0:T(8,128)(2,1)S(1)} %fusion.5) | copy-start | bytes 6291460
  24.6 5.0 %copy-start.4 = (bf16[1,16,128,512]{3,2,1,0:T(8,128)(2,1)S(1)}, bf16[1,16,128,512]{3,2,1,0:T(8,128)(2,1)}, u32[]{:S(2)}) copy-start(bf16[1,16,128,512]{3,2,1,0:T(8,128)(2,1)} %copy.25) | copy-start | bytes 6291460
  50.5 3.7 copy-start.13
  50.5 5.0 %copy-start.12 = (s32[1,16]{1,0:T(1,128)S(1)}, s32[1,16]{1,0:T(1,128)}, u32[]{:S(2)}) copy-start(s32[1,16]{1,0:T(1,128)} %param.10) | copy-start | bytes 196
  50.5 130.5 %copy-start.11 = (s32[1,16]{1,0:T(1,128)S(1)}, s32[1,16]{1,0:T(1,128)}, u32[]{:S(2)}) copy-start(s32[1,16]{1,0:T(1,128)} %param.11) | copy-start | bytes 196
  96.1 368.8 %all-reduce.7.cloned.1.call-start = ((), (), s32[]{:S(2)}) async-start(), calls=%async_computation.2 | async-start | bytes 6815744 | tf_op jit(solution)/shard_map/psum | solution.py:144
  179.9 8.1 %copy-start.1 = (f32[2048,512]{1,0:T(8,128)S(1)}, f32[2048,512]{1,0:T(8,128)}, u32[]{:S(2)}) copy-start(f32[2048,512]{1,0:T(8,128)} %add_add_fusion) | copy-start | bytes 12582916
  188.0 2.7 copy-start.6
  190.8 3.7 copy-start.2
  192.1 2.4 copy-start.7
  197.7 3.1 copy-start.3
  197.7 3.1 copy-start.8
  464.9 3.9 copy-start.9
Sparse Core Ops, SparseCore 0:
  96.2 83.6 reduce-scatter.1
  197.8 267.0 all-reduce.6
where the time goes:
time: 478 us; the launch traced here: 476 us
  waiting for transfers between devices  266 us (56%)
  blocking collectives  117 us (24%)
  matrix products  31.8 us (7%)
  local copies, waits for them, and re-layouts  28.6 us (6%)
  other arithmetic  17.9 us (4%)
  between operations  15 us (3%)
    psum x1, waiting for transfers between devices, body(): grads = lax.psum((grads[0], grads[1], grads[2]), ('row', 'grp'))  182 us
    reduce_scatter x1, waiting for transfers between devices, body(): lax.psum_scatter(lax.dot_general(softmax, encounter_latent_vector, (((0,)...  83.6 us
    psum x1, blocking collectives, body(): grads = lax.psum((grads[0], grads[1], grads[2]), ('row', 'grp'))  77.7 us
    all_gather x1, blocking collectives, body(): lax.all_gather(encounter_latent_vector, 'row', axis=0, tiled=True)  27.9 us
    dot_general x3, matrix products, encode(): jnp.dot(shifted_input, conv_weight[filter_tap_index], preferred_element_t...  16.7 us
    unnamed x1, blocking collectives  11.1 us
    slice x3, local copies, waits for them, and re-layouts, filter_tap_window(): padded[:, filter_tap_index * spacing:filter_tap_index * spacing + sequenc...  11 us
  transfers between devices with their start and end apart: 2, of which 2 were waited for; matrix products, arithmetic and copies ran while one was open for 1% of the time, Pallas kernels for 0%

commit v1 on v0

v1 whole, which is shorter than its diff:
```python
import functools

import jax
import jax.numpy as jnp
from jax import lax
from jax.experimental import pallas as pl
from jax.experimental.pallas import tpu as pltpu
from jax.sharding import Mesh, PartitionSpec as P

GAP = 2
TEMPERATURE = 0.1
EPS = 1e-05
HIGHEST = lax.Precision.HIGHEST

SEGS = 16
LEN = 128
C = 512
PROJ = 128
TAPS = 3
STEP_SEGS = 4
ROWS = STEP_SEGS * LEN
STEPS = SEGS // STEP_SEGS

RANKS = 8
PLANE = 16
DEPTH = 8
BLOCKS = TAPS * C // 128
HALF = BLOCKS // 2
CONV_ROWS = HALF * (C // PLANE)
PROJ_ROWS = C // 2 // PLANE
CHUNK = CONV_ROWS + PROJ_ROWS
GAIN_ROWS = 8
Z_CONV = CONV_ROWS // DEPTH
Z_PROJ = PROJ_ROWS // DEPTH
Z_CHUNK = 32

VMEM = pltpu.VMEM
SMEM = pltpu.SMEM


def whole(shape, space=None):
    zeros = (0,) * len(shape)
    return pl.BlockSpec(shape, lambda *_: zeros, memory_space=space)


def later(rows):
    return jnp.concatenate([rows[GAP:], jnp.zeros((GAP, rows.shape[1]), rows.dtype)], axis=0)


def earlier(rows):
    return jnp.concatenate([jnp.zeros((GAP, rows.shape[1]), rows.dtype), rows[:-GAP]], axis=0)


def unit_rows(values):
    return values * lax.rsqrt(jnp.mean(values * values, axis=-1, keepdims=True) + EPS)


def forward_kernel(
    group, segments, weight, gain, head, normed_out, slope_out, pooled_out, projected_out, send_out, pooled
):
    step = pl.program_id(0)
    cubic = 0.044715
    scale = 0.7978845608028654
    for index in range(STEP_SEGS):
        inputs = segments[0, index].astype(jnp.float32)
        normed = (unit_rows(inputs) * gain[...]).astype(jnp.bfloat16)
        normed_out[index * LEN : (index + 1) * LEN, :] = normed
        conv = jnp.dot(earlier(normed), weight[0], preferred_element_type=jnp.float32)
        conv += jnp.dot(normed, weight[1], preferred_element_type=jnp.float32)
        conv += jnp.dot(later(normed), weight[2], preferred_element_type=jnp.float32)
        square = conv * conv
        bent = jnp.tanh(conv * (scale + (scale * cubic) * square))
        half = 0.5 + 0.5 * bent
        hidden = inputs + conv * half
        slope_out[index * LEN : (index + 1) * LEN, :] = half + (0.5 * conv) * (1.0 - bent * bent) * (
            scale + (3.0 * scale * cubic) * square
        )
        pooled[pl.ds(step * STEP_SEGS + index, 1), :] = jnp.sum(hidden, axis=0, keepdims=True) * (1.0 / LEN)

    @pl.when(step == STEPS - 1)
    def _():
        rounded = pooled[...].astype(jnp.bfloat16)
        pooled_out[...] = rounded
        projected = jnp.dot(rounded, head[...], preferred_element_type=jnp.float32)
        projected_out[...] = projected
        embedding = unit_rows(projected) * PROJ ** (-0.5)
        lane = lax.broadcasted_iota(jnp.int32, (8, 128), 1) & (SEGS - 1)
        groups = jnp.zeros((8, 128), jnp.int32)
        for index in range(SEGS):
            groups = jnp.where(lane == index, group[0, index], groups)
        groups = groups.astype(jnp.float32)
        for rank in range(RANKS):
            send_out[rank, 0:SEGS, :] = embedding
            send_out[rank, SEGS:, :] = groups


def forward(group, segments, weight, gain, head):
    f32 = jnp.float32
    return pl.pallas_call(
        forward_kernel,
        grid=(STEPS,),
        in_specs=[
            whole((1, SEGS), SMEM),
            pl.BlockSpec((1, STEP_SEGS, LEN, C), lambda i: (0, i, 0, 0)),
            whole((TAPS, C, C)),
            whole((1, C)),
            whole((C, PROJ)),
        ],
        out_specs=[
            pl.BlockSpec((ROWS, C), lambda i: (i, 0)),
            pl.BlockSpec((ROWS, C), lambda i: (i, 0)),
            whole((SEGS, C)),
            whole((SEGS, PROJ)),
            whole((RANKS, SEGS + 8, PROJ)),
        ],
        out_shape=[
            jax.ShapeDtypeStruct((SEGS * LEN, C), jnp.bfloat16),
            jax.ShapeDtypeStruct((SEGS * LEN, C), f32),
            jax.ShapeDtypeStruct((SEGS, C), jnp.bfloat16),
            jax.ShapeDtypeStruct((SEGS, PROJ), f32),
            jax.ShapeDtypeStruct((RANKS, SEGS + 8, PROJ), f32),
        ],
        scratch_shapes=[VMEM((SEGS, C), f32)],
        compiler_params=pltpu.CompilerParams(vmem_limit_bytes=48 << 20),
        cost_estimate=pl.CostEstimate(flops=2 * SEGS * LEN * TAPS * C * C, bytes_accessed=10 << 20, transcendentals=SEGS * LEN * C),
        name="forward",
    )(group, segments, weight, gain, head)


def loss_gradient(positive, gathered, projected, pooled, head, partner, place):
    embeddings = gathered[:, 0:SEGS, :].reshape(RANKS * SEGS, PROJ)
    own = unit_rows(projected[...]) * PROJ ** (-0.5)
    count = RANKS * SEGS
    nt = (((1,), (1,)), ((), ()))
    lane = lax.broadcasted_iota(jnp.int32, (8, 128), 1)
    groups = jnp.zeros((8, 128), jnp.float32)
    for rank in range(RANKS):
        groups = jnp.where(lane >> 4 == rank, gathered[rank, SEGS:, :], groups)
    by_column = jnp.broadcast_to(groups[0:1], (count, count))
    by_row = by_column.T
    row = lax.broadcasted_iota(jnp.int32, (count, count), 0)
    column = lax.broadcasted_iota(jnp.int32, (count, count), 1)
    same = (by_row == by_column) & (row != column)
    scores = lax.dot_general(
        embeddings, embeddings, nt, precision=HIGHEST, preferred_element_type=jnp.float32
    ) / TEMPERATURE
    column_total = jnp.log(jnp.sum(jnp.where(same, jnp.exp(scores), 0.0), axis=0, keepdims=True))

    own_scores = lax.dot_general(
        own, embeddings, nt, precision=HIGHEST, preferred_element_type=jnp.float32
    ) / TEMPERATURE
    own_row = lax.broadcasted_iota(jnp.int32, (SEGS, count), 0) + place * SEGS
    own_column = lax.broadcasted_iota(jnp.int32, (SEGS, count), 1)
    own_group = jnp.sum(jnp.where(own_row == own_column, groups[0:1], 0.0), axis=1, keepdims=True)
    own_same = (own_group == groups[0:1]) & (own_row != own_column)
    own_total = jnp.log(jnp.sum(jnp.where(own_same, jnp.exp(own_scores), 0.0), axis=1, keepdims=True))
    both = jnp.where(own_same, jnp.exp(own_scores - own_total) + jnp.exp(own_scores - column_total), 0.0)
    pulled = jnp.dot(both, embeddings, precision=HIGHEST, preferred_element_type=jnp.float32)
    for index in range(SEGS):
        where = positive[0, index]
        partner[index : index + 1, :] = gathered[where >> 4, pl.ds(where & (SEGS - 1), 1), :]
    factor = (count * 32) ** (-0.5) / TEMPERATURE
    embed_grad = factor * (pulled - 2.0 * partner[...])

    values = projected[...]
    inverse = lax.rsqrt(jnp.mean(values * values, axis=-1, keepdims=True) + EPS)
    outer = embed_grad * PROJ ** (-0.5)
    dotted = jnp.mean(values * outer, axis=-1, keepdims=True)
    projected_grad = inverse * outer - values * (inverse * inverse * inverse * dotted)
    derivative = lax.dot_general(
        pooled[...].astype(jnp.float32),
        projected_grad,
        (((0,), (0,)), ((), ())),
        precision=HIGHEST,
        preferred_element_type=jnp.float32,
    )
    hidden_grad = lax.dot_general(
        projected_grad, head[...].astype(jnp.float32), nt, precision=HIGHEST, preferred_element_type=jnp.float32
    ) * (1.0 / LEN)
    return derivative, hidden_grad


def weight_kernel(
    places, positive, gathered, projected, pooled, head, normed, slope, grad_out, keep_out, send_out,
    total, hidden_grad, derivative, partner,
):
    step = pl.program_id(0)

    @pl.when(step == 0)
    def _():
        derivative[...], hidden_grad[...] = loss_gradient(
            positive, gathered, projected, pooled, head, partner, places[0]
        )
        total[...] = jnp.zeros_like(total)

    shifted = []
    for index in range(STEP_SEGS):
        span = slice(index * LEN, (index + 1) * LEN)
        grad = (hidden_grad[pl.ds(step * STEP_SEGS + index, 1), :] * slope[span, :]).astype(jnp.bfloat16)
        grad_out[span, :] = grad
        shifted.append((later(grad), grad, earlier(grad)))
    rows = normed[...]
    for tap in range(TAPS):
        side = jnp.concatenate([parts[tap] for parts in shifted], axis=0)
        product = lax.dot_general(
            rows, side, (((0,), (0,)), ((), ())), preferred_element_type=jnp.float32
        )
        for block in range(C // 128):
            total[tap * (C // 128) + block] += product[:, block * 128 : (block + 1) * 128]

    @pl.when(step == STEPS - 1)
    def _():
        core = places[1]
        each = C // PLANE
        for target, which in ((keep_out, core), (send_out, 1 - core)):
            for chunk in range(PLANE):
                for block in range(HALF):
                    target[chunk, block * each : (block + 1) * each, :] = total[
                        which * HALF + block, chunk * each : (chunk + 1) * each, :
                    ]
                target[chunk, CONV_ROWS:, :] = derivative[
                    pl.ds(pl.multiple_of(which * (C // 2) + chunk * PROJ_ROWS, PROJ_ROWS), PROJ_ROWS), :
                ]


def weight_gradient(places, positive, gathered, projected, pooled, head, normed, slope):
    f32 = jnp.float32
    return pl.pallas_call(
        weight_kernel,
        grid=(STEPS,),
        in_specs=[
            whole((2,), SMEM),
            whole((1, SEGS), SMEM),
            whole((RANKS, SEGS + 8, PROJ)),
            whole((SEGS, PROJ)),
            whole((SEGS, C)),
            whole((C, PROJ)),
            pl.BlockSpec((ROWS, C), lambda i: (i, 0)),
            pl.BlockSpec((ROWS, C), lambda i: (i, 0)),
        ],
        out_specs=[
            pl.BlockSpec((ROWS, C), lambda i: (i, 0)),
            whole((PLANE, CHUNK, 128)),
            whole((PLANE, CHUNK, 128)),
        ],
        out_shape=[
            jax.ShapeDtypeStruct((SEGS * LEN, C), jnp.bfloat16),
            jax.ShapeDtypeStruct((PLANE, CHUNK, 128), f32),
            jax.ShapeDtypeStruct((PLANE, CHUNK, 128), f32),
        ],
        scratch_shapes=[
            VMEM((BLOCKS, C, 128), f32),
            VMEM((SEGS, C), f32),
            VMEM((C, PROJ), f32),
            VMEM((SEGS, PROJ), f32),
        ],
        compiler_params=pltpu.CompilerParams(vmem_limit_bytes=48 << 20),
        cost_estimate=pl.CostEstimate(flops=2 * SEGS * LEN * TAPS * C * C, bytes_accessed=12 << 20, transcendentals=1 << 16),
        name="weight_gradient",
    )(places, positive, gathered, projected, pooled, head, normed, slope)


def gain_kernel(grad, segments, weight, out, total):
    step = pl.program_id(0)

    @pl.when(step == 0)
    def _():
        total[...] = jnp.zeros_like(total)

    nt = (((1,), (1,)), ((), ()))
    for index in range(STEP_SEGS):
        middle = grad[index * LEN : (index + 1) * LEN, :]
        normed_grad = lax.dot_general(later(middle), weight[0], nt, preferred_element_type=jnp.float32)
        normed_grad += lax.dot_general(middle, weight[1], nt, preferred_element_type=jnp.float32)
        normed_grad += lax.dot_general(earlier(middle), weight[2], nt, preferred_element_type=jnp.float32)
        product = normed_grad * unit_rows(segments[0, index].astype(jnp.float32))
        total[...] += jnp.sum(product.reshape(LEN // 8, 8, C), axis=0)

    @pl.when(step == STEPS - 1)
    def _():
        summed = jnp.sum(total[...], axis=0, keepdims=True)
        for block in range(GAIN_ROWS):
            at = block % (C // 128)
            out[block : block + 1, :] = summed[:, at * 128 : (at + 1) * 128]


def gain_gradient(grad, segments, weight):
    f32 = jnp.float32
    return pl.pallas_call(
        gain_kernel,
        grid=(STEPS,),
        in_specs=[
            pl.BlockSpec((ROWS, C), lambda i: (i, 0)),
            pl.BlockSpec((1, STEP_SEGS, LEN, C), lambda i: (0, i, 0, 0)),
            whole((TAPS, C, C)),
        ],
        out_specs=whole((GAIN_ROWS, 128)),
        out_shape=jax.ShapeDtypeStruct((GAIN_ROWS, 128), f32),
        scratch_shapes=[VMEM((8, C), f32)],
        compiler_params=pltpu.CompilerParams(vmem_limit_bytes=48 << 20),
        cost_estimate=pl.CostEstimate(flops=2 * SEGS * LEN * TAPS * C * C, bytes_accessed=6 << 20, transcendentals=0),
        name="gain_gradient",
    )(grad, segments, weight)


def small_call(body, out_shape, name, *args):
    return pl.pallas_call(
        body,
        out_shape=out_shape,
        compiler_params=pltpu.CompilerParams(vmem_limit_bytes=24 << 20),
        cost_estimate=pl.CostEstimate(flops=1 << 20, bytes_accessed=4 << 20, transcendentals=0),
        name=name,
    )(*args)


def pair_sum_kernel(keep, received, gain, out):
    for chunk in range(PLANE):
        out[chunk, 0:CHUNK, :] = keep[chunk] + received[chunk]
        out[chunk, CHUNK:, :] = gain[...]


def plane_sum_kernel(received, out):
    summed = received[0]
    for source in range(1, PLANE):
        summed = summed + received[source]
    for depth in range(DEPTH):
        out[depth, 0:Z_CONV, :] = summed[depth * Z_CONV : (depth + 1) * Z_CONV, :]
        out[depth, Z_CONV : Z_CONV + Z_PROJ, :] = summed[
            CONV_ROWS + depth * Z_PROJ : CONV_ROWS + (depth + 1) * Z_PROJ, :
        ]
        out[depth, Z_CONV + Z_PROJ :, :] = summed[CHUNK : CHUNK + Z_CHUNK - Z_CONV - Z_PROJ, :]


def depth_sum_kernel(received, out, gain_out):
    summed = received[0]
    for source in range(1, DEPTH):
        summed = summed + received[source]
    for depth in range(DEPTH):
        out[depth] = summed
    gain_out[...] = summed[Z_CONV:, :]


def spread_kernel(received, out):
    for chunk in range(PLANE):
        for depth in range(DEPTH):
            out[chunk, depth * Z_CONV : (depth + 1) * Z_CONV, :] = received[depth, 0:Z_CONV, :]
            out[chunk, CONV_ROWS + depth * Z_PROJ : CONV_ROWS + (depth + 1) * Z_PROJ, :] = received[
                depth, Z_CONV : Z_CONV + Z_PROJ, :
            ]


def place_kernel(places, mine, other, gain_mine, gain_other, conv_out, gain_out, head_out):
    each = C // PLANE
    wide = C // 128
    first = places[1] == 0
    for chunk in range(PLANE):
        for half in range(2):
            rows = jnp.where(first == (half == 0), mine[chunk], other[chunk])
            for block in range(HALF):
                at = half * HALF + block
                conv_out[
                    at // wide, chunk * each : (chunk + 1) * each, (at % wide) * 128 : (at % wide + 1) * 128
                ] = rows[block * each : (block + 1) * each, :]
            start = half * (C // 2) + chunk * PROJ_ROWS
            head_out[start : start + PROJ_ROWS, :] = rows[CONV_ROWS:, :]
    summed = gain_mine[...] + gain_other[...]
    gain_out[...] = summed[Z_PROJ : Z_PROJ + wide, :]


def body(segments, conv_weight, gain, head, group, positive):
    f32 = jnp.float32
    plane = ("x", "yh", "yl")
    swap = [(0, 1), (1, 0)]
    places = jnp.stack([lax.axis_index(("x", "yh")), lax.axis_index("core")]).astype(jnp.int32)
    normed, slope, pooled, projected, send = forward(group, segments, conv_weight, gain.reshape(1, C), head)
    gathered = lax.all_to_all(send, ("x", "yh"), 0, 0)
    grad, keep, give = weight_gradient(places, positive, gathered, projected, pooled, head, normed, slope)
    received = lax.ppermute(give, "core", swap)
    gain_part = gain_gradient(grad, segments, conv_weight)
    paired = small_call(
        pair_sum_kernel, jax.ShapeDtypeStruct((PLANE, CHUNK + GAIN_ROWS, 128), f32), "pair_sum", keep, received, gain_part
    )
    across = lax.all_to_all(paired, plane, 0, 0)
    summed = small_call(plane_sum_kernel, jax.ShapeDtypeStruct((DEPTH, Z_CHUNK, 128), f32), "plane_sum", across)
    along = lax.all_to_all(summed, "z", 0, 0)
    done, gain_mine = small_call(
        depth_sum_kernel,
        (jax.ShapeDtypeStruct((DEPTH, Z_CHUNK, 128), f32), jax.ShapeDtypeStruct((8, 128), f32)),
        "depth_sum",
        along,
    )
    gain_other = lax.ppermute(gain_mine, "core", swap)
    back = lax.all_to_all(done, "z", 0, 0)
    spread = small_call(spread_kernel, jax.ShapeDtypeStruct((PLANE, CHUNK, 128), f32), "spread", back)
    mine = lax.all_to_all(spread, plane, 0, 0)
    other = lax.ppermute(mine, "core", swap)
    conv_grad, gain_grad, head_grad = pl.pallas_call(
        place_kernel,
        in_specs=[pl.BlockSpec(memory_space=SMEM)] + [pl.BlockSpec(memory_space=VMEM)] * 4,
        out_shape=(
            jax.ShapeDtypeStruct((TAPS, C, C), f32),
            jax.ShapeDtypeStruct((C // 128, 128), f32),
            jax.ShapeDtypeStruct((C, PROJ), f32),
        ),
        compiler_params=pltpu.CompilerParams(vmem_limit_bytes=24 << 20),
        name="place",
    )(places, mine, other, gain_mine, gain_other)
    return conv_grad, gain_grad.reshape(C), head_grad


def solution(mesh):
    fine = Mesh(mesh.devices.reshape(4, 2, 8, 2, 2), ("x", "yh", "z", "yl", "core"))
    row, grp = ("x", "yh"), ("z", "yl", "core")
    placed = (P(grp, row, None, None), P(), P(), P(), P(grp, row), P(grp, row))
    return jax.shard_map(body, mesh=fine, in_specs=placed, out_specs=(P(), P(), P()), check_vma=False)
```

time: 478 us -> 137 us (0.29)
  waiting for transfers between devices: 266 us -> 9.81 us
  blocking collectives: 117 us -> 77 us
  matrix products: 31.8 us -> 0 us
  Pallas kernels: 0 us -> 28.4 us
  local copies, waits for them, and re-layouts: 28.6 us -> 6.57 us
  other arithmetic: 17.9 us -> 0.07 us
  between operations: 15 us -> 0.7 us
  starting transfers between devices: 0.26 us -> 14.4 us
    psum x1 -> x0, waiting for transfers between devices: 182 us -> none  [body(): grads = lax.psum((grads[0], grads[1], grads[2]), ('row', 'grp'))]
    reduce_scatter x1 -> x0, waiting for transfers between devices: 83.6 us -> none  [body(): lax.psum_scatter(lax.dot_general(softmax, encounter_latent_vector, (((0,)...]
    psum x1 -> x0, blocking collectives: 77.7 us -> none  [body(): grads = lax.psum((grads[0], grads[1], grads[2]), ('row', 'grp'))]
    all_to_all x0 -> x4, blocking collectives: none -> 77 us  [the longest x1 26.8 us: body(): across = lax.all_to_all(paired, plane, 0, 0)]
    dot_general x16 -> x0, matrix products: 31.8 us -> none  [the longest x3 16.7 us: encode(): jnp.dot(shifted_input, conv_weight[filter_tap_index], preferred_element_t...]
    pallas_call x0 -> x8, Pallas kernels: none -> 28.4 us  [the longest x1 8.84 us: gain_gradient(): pl.pallas_call(gain_kernel, grid=(STEPS,), in_specs=[pl.BlockSpec((ROWS,...]
    all_gather x1 -> x0, blocking collectives: 27.9 us -> none  [body(): lax.all_gather(encounter_latent_vector, 'row', axis=0, tiled=True)]
    convert_element_type x4 -> x0, other arithmetic: 11.9 us -> none  [the longest x2 9.15 us: backward(): jax.vjp(partial(jax.nn.gelu, approximate=True), conv)[1](hidden_grad)[0]]
  transfers between devices with their start and end apart: 2 -> 4, of which waited for: 2 -> 2; matrix products, arithmetic and copies ran while one was open for 1% -> 0% of each run, Pallas kernels for 0% -> 6%
where the time goes in v1:
time: 137 us
  blocking collectives  77 us (56%)
  Pallas kernels  28.4 us (21%)
  starting transfers between devices  14.4 us (11%)
  waiting for transfers between devices  9.81 us (7%)
  local copies, waits for them, and re-layouts  6.57 us (5%)
    all_to_all x1, blocking collectives, body(): across = lax.all_to_all(paired, plane, 0, 0)  26.8 us
    all_to_all x1, blocking collectives, body(): mine = lax.all_to_all(spread, plane, 0, 0)  24 us
    all_to_all x1, blocking collectives, body(): along = lax.all_to_all(summed, 'z', 0, 0)  15.9 us
    all_to_all x1, blocking collectives, body(): back = lax.all_to_all(done, 'z', 0, 0)  10.3 us
    pallas_call x1, Pallas kernels, gain_gradient(): pl.pallas_call(gain_kernel, grid=(STEPS,), in_specs=[pl.BlockSpec((ROWS,...  8.84 us
    pallas_call x1, Pallas kernels, forward(): pl.pallas_call(forward_kernel, grid=(STEPS,), in_specs=[whole((1, SEGS),...  8.7 us
    pallas_call x1, Pallas kernels, weight_gradient(): pl.pallas_call(weight_kernel, grid=(STEPS,), in_specs=[whole((2,), SMEM),...  7.94 us
    all_to_all x1, starting transfers between devices, body(): gathered = lax.all_to_all(send, ('x', 'yh'), 0, 0)  7.47 us
  transfers between devices with their start and end apart: 4, of which 2 were waited for; matrix products, arithmetic and copies ran while one was open for 0% of the time, Pallas kernels for 6%

profile of v1, /device:TPU:1, one launch (start us, length us, event | category | flops | bytes accessed | tf_op | source)
XLA Modules:
  0.0 137.0 jit_solution(1865785306686495371)
XLA Ops:
  0.6 0.0 copy-start
  0.6 1.6 %copy-done = bf16[1,16,128,512]{3,2,1,0:T(8,128)(2,1)S(1)} copy-done((bf16[1,16,128,512]{3,2,1,0:T(8,128)(2,1)S(1)}, bf16[1,16,128,512]{3,2,1,0:T(8,128)(2,1)}, u32[]{:S(2)}) %copy-start) | copy-done | bytes 2097176
  2.2 0.0 copy-start.2
  2.2 1.4 %copy-done.2 = bf16[3,512,512]{2,1,0:T(8,128)(2,1)S(1)} copy-done((bf16[3,512,512]{2,1,0:T(8,128)(2,1)S(1)}, bf16[3,512,512]{2,1,0:T(8,128)(2,1)}, u32[]{:S(2)}) %copy-start.2) | copy-done | bytes 1572888
  3.6 0.0 copy-start.4
  3.6 0.9 copy-done.4
  4.5 0.0 copy-start.6
  4.5 0.7 copy-done.6
  5.2 0.0 copy-start.7
  5.2 0.7 copy-done.7
  5.9 0.0 copy-start.5
  5.9 0.0 copy-start.8
  5.9 8.7 %forward.1 = (bf16[2048,512]{1,0:T(8,128)(2,1)S(1)}, f32[2048,512]{1,0:T(8,128)}, bf16[16,512]{1,0:T(8,128)(2,1)S(1)}, f32[16,128]{1,0:T(8,128)S(1)}, f32[8,24,128]{2,1,0:T(8,128)}) custom-call(s32[1,16]{1,0:T(1,128)S(1)} %copy-done.7, bf16[1,16,128,512]{3,2,1,0:T(8,128)(2,1)S(1)} %copy-done, bf16[3,512,512]{2,1,0:T(8,128)(2,1)S(1)} %copy-done.2, ...), custom_call_target="tpu_custom_call" | custom-call | flops 3221225472 | bytes 10485760 | tf_op jit(solution)/shard_map/forward/pallas_call | solution.py:99
  14.6 0.0 copy-start.9
  14.6 1.3 copy-done.9
  15.9 7.5 %all-to-all-start = ((f32[8,24,128]{2,1,0:T(8,128)}), f32[8,24,128]{2,1,0:T(8,128)S(1)}, u32[]{:S(2)}, u32[]{:S(2)}) async-start(f32[8,24,128]{2,1,0:T(8,128)} %get-tuple-element.16), calls=%async_computation | async-start | bytes 196608 | tf_op jit(solution)/shard_map/all_to_all | solution.py:376
  23.4 0.1 pad_add_fusion.places
  23.4 6.6 %all-to-all-done.gathered = f32[8,24,128]{2,1,0:T(8,128)S(1)} async-done(((f32[8,24,128]{2,1,0:T(8,128)}), f32[8,24,128]{2,1,0:T(8,128)S(1)}, u32[]{:S(2)}, u32[]{:S(2)}) %all-to-all-start) | async-done | bytes 98336 | tf_op jit(solution)/shard_map/all_to_all | solution.py:376
  30.0 0.0 copy-done.5
  30.0 0.0 copy-done.8
  30.0 0.0 copy-start.1
  30.0 0.0 copy-start.3
  30.0 7.9 %weight_gradient.1 = (bf16[2048,512]{1,0:T(8,128)(2,1)S(1)}, f32[16,208,128]{2,1,0:T(8,128)S(1)}, f32[16,208,128]{2,1,0:T(8,128)S(1)}) custom-call(s32[2]{0:T(128)S(1)} %pad_add_fusion.places, s32[1,16]{1,0:T(1,128)S(1)} %copy-done.8, f32[8,24,128]{2,1,0:T(8,128)S(1)} %all-to-all-done.gathered, f32[16,128]{1,0:T(8,128)S(1)} %get-tuple-element.17.projected, ...), custom_call_target="tpu_custom_call" | custom-call | flops 3221225472 | bytes 12582912 | tf_op jit(solution)/shard_map/weight_gradient/pallas_call | solution.py:228
  38.0 2.2 %collective-permute-start = (f32[16,208,128]{2,1,0:T(8,128)S(1)}, f32[16,208,128]{2,1,0:T(8,128)S(1)}, u32[]{:S(2)}, u32[]{:S(2)}) collective-permute-start(f32[16,208,128]{2,1,0:T(8,128)S(1)} %get-tuple-element.22), channel_id=1, source_target_pairs={{0,1},{1,0},{2,3},{3,2},{4,5},{5,4},{6,7},{7,6},{8,9},{9,8},{10,11... | collective-permute-start | bytes 5111816 | tf_op jit(solution)/shard_map/ppermute | solution.py:378
  40.2 0.0 copy-done.1
  40.2 0.0 copy-done.3
  40.2 8.8 %gain_gradient.1.gain = f32[8,128]{1,0:T(8,128)S(1)} custom-call(bf16[2048,512]{1,0:T(8,128)(2,1)S(1)} %get-tuple-element.23.grad, bf16[1,16,128,512]{3,2,1,0:T(8,128)(2,1)S(1)} %copy-done.1, bf16[3,512,512]{2,1,0:T(8,128)(2,1)S(1)} %copy-done.3), custom_call_target="tpu_custom_call" | custom-call | flops 3221225472 | bytes 6291456 | tf_op jit(solution)/shard_map/gain_gradient/pallas_call | solution.py:289
  49.0 0.0 collective-permute-done.received
  49.0 0.2 pair_sum.1
  49.2 26.8 %all_to_all.25.received = f32[16,216,128]{2,1,0:T(8,128)S(1)} all-to-all(f32[16,216,128]{2,1,0:T(8,128)S(1)} %pair_sum.1), channel_id=1, replica_groups=mesh['x'=4,'yh'=2,'z'=8,'yl'=2,'core'=2] {'x','yh','yl'}, dimensions={0} | all-to-all | bytes 3538944 | tf_op jit(solution)/shard_map/all_to_all | solution.py:383
  76.0 0.1 plane_sum.1
  76.1 15.9 %all_to_all.26.received = f32[8,32,128]{2,1,0:T(8,128)S(1)} all-to-all(f32[8,32,128]{2,1,0:T(8,128)S(1)} %plane_sum.1), channel_id=1, replica_groups=mesh['x'=4,'yh'=2,'z'=8,'yl'=2,'core'=2] {'z'}, dimensions={0} | all-to-all | bytes 262144 | tf_op jit(solution)/shard_map/all_to_all | solution.py:385
  92.0 10.3 %all_to_all.27.received = f32[8,32,128]{2,1,0:T(8,128)S(1)} all-to-all(f32[8,32,128]{2,1,0:T(8,128)S(1)} %get-tuple-element.24), channel_id=1, replica_groups=mesh['x'=4,'yh'=2,'z'=8,'yl'=2,'core'=2] {'z'}, dimensions={0} | all-to-all | bytes 262144 | tf_op jit(solution)/shard_map/all_to_all | solution.py:393
  102.3 0.1 spread.1
  102.5 24.0 %all_to_all.28.mine = f32[16,208,128]{2,1,0:T(8,128)S(1)} all-to-all(f32[16,208,128]{2,1,0:T(8,128)S(1)} %spread.1), channel_id=1, replica_groups=mesh['x'=4,'yh'=2,'z'=8,'yl'=2,'core'=2] {'x','yh','yl'}, dimensions={0} | all-to-all | bytes 3407872 | tf_op jit(solution)/shard_map/all_to_all | solution.py:395
  126.5 4.8 %collective-permute-start.1 = (f32[16,208,128]{2,1,0:T(8,128)S(1)}, f32[16,208,128]{2,1,0:T(8,128)S(1)}, u32[]{:S(2)}, u32[]{:S(2)}) collective-permute-start(f32[16,208,128]{2,1,0:T(8,128)S(1)} %all_to_all.28.mine), channel_id=1, source_target_pairs={{0,1},{1,0},{2,3},{3,2},{4,5},{5,4},{6,7},{7,6},{8,9},{9,8},{10,11... | collective-permute-start | bytes 5111816 | tf_op jit(solution)/shard_map/ppermute | solution.py:396
  131.3 0.0 collective-permute-start.2
  131.3 3.2 %collective-permute-done.2.gain_other = f32[8,128]{1,0:T(8,128)S(1)} collective-permute-done((f32[8,128]{1,0:T(8,128)S(1)}, f32[8,128]{1,0:T(8,128)S(1)}, u32[]{:S(2)}, u32[]{:S(2)}) %collective-permute-start.2) | collective-permute-done | bytes 4128 | tf_op jit(solution)/shard_map/ppermute | solution.py:392
  134.5 0.0 collective-permute-done.1.other
  134.5 2.5 %place.1 = (f32[3,512,512]{2,1,0:T(8,128)}, f32[4,128]{1,0:T(4,128)}, f32[512,128]{1,0:T(8,128)}) custom-call(s32[2]{0:T(128)S(1)} %pad_add_fusion.places, f32[16,208,128]{2,1,0:T(8,128)S(1)} %all_to_all.28.mine, f32[16,208,128]{2,1,0:T(8,128)S(1)} %collective-permute-done.1.other, f32[8,128]{1,0:T(8,128)S(1)} %get-tuple-element.25.gain_mine, ...), custom_call_target="tpu_custom_call" | custom-call | tf_op jit(solution)/shard_map/place/pallas_call | solution.py:397
  (1 shorter events, 0.0 us)
Async XLA Ops:
  0.6 1.6 %copy-start = (bf16[1,16,128,512]{3,2,1,0:T(8,128)(2,1)S(1)}, bf16[1,16,128,512]{3,2,1,0:T(8,128)(2,1)}, u32[]{:S(2)}) copy-start(bf16[1,16,128,512]{3,2,1,0:T(8,128)(2,1)} %segments.3) | copy-start | bytes 6291460
  2.2 1.4 %copy-start.2 = (bf16[3,512,512]{2,1,0:T(8,128)(2,1)S(1)}, bf16[3,512,512]{2,1,0:T(8,128)(2,1)}, u32[]{:S(2)}) copy-start(bf16[3,512,512]{2,1,0:T(8,128)(2,1)} %weight.3) | copy-start | bytes 4718596
  3.6 0.9 copy-start.4
  4.5 0.7 copy-start.6
  5.2 0.7 copy-start.7
  5.9 24.2 %copy-start.5 = (bf16[512,128]{1,0:T(8,128)(2,1)S(1)}, bf16[512,128]{1,0:T(8,128)(2,1)}, u32[]{:S(2)}) copy-start(bf16[512,128]{1,0:T(8,128)(2,1)} %head.3) | copy-start | bytes 393220
  5.9 24.2 %copy-start.8 = (s32[1,16]{1,0:T(1,128)S(1)}, s32[1,16]{1,0:T(1,128)}, u32[]{:S(2)}) copy-start(s32[1,16]{1,0:T(1,128)} %positive.1) | copy-start | bytes 196
  14.6 1.3 copy-start.9
  15.9 14.1 %all-to-all-start = ((f32[8,24,128]{2,1,0:T(8,128)}), f32[8,24,128]{2,1,0:T(8,128)S(1)}, u32[]{:S(2)}, u32[]{:S(2)}) async-start(f32[8,24,128]{2,1,0:T(8,128)} %get-tuple-element.16), calls=%async_computation | async-start | bytes 196608 | tf_op jit(solution)/shard_map/all_to_all | solution.py:376
  30.0 10.1 %copy-start.1 = (bf16[1,16,128,512]{3,2,1,0:T(8,128)(2,1)S(1)}, bf16[1,16,128,512]{3,2,1,0:T(8,128)(2,1)}, u32[]{:S(2)}) copy-start(bf16[1,16,128,512]{3,2,1,0:T(8,128)(2,1)} %segments.3) | copy-start | bytes 6291460
  30.0 10.1 %copy-start.3 = (bf16[3,512,512]{2,1,0:T(8,128)(2,1)S(1)}, bf16[3,512,512]{2,1,0:T(8,128)(2,1)}, u32[]{:S(2)}) copy-start(bf16[3,512,512]{2,1,0:T(8,128)(2,1)} %weight.3) | copy-start | bytes 4718596
  38.0 11.0 %collective-permute-start = (f32[16,208,128]{2,1,0:T(8,128)S(1)}, f32[16,208,128]{2,1,0:T(8,128)S(1)}, u32[]{:S(2)}, u32[]{:S(2)}) collective-permute-start(f32[16,208,128]{2,1,0:T(8,128)S(1)} %get-tuple-element.22), channel_id=1, source_target_pairs={{0,1},{1,0},{2,3},{3,2},{4,5},{5,4},{6,7},{7,6},{8,9},{9,8},{10,11... | collective-permute-start | bytes 5111816 | tf_op jit(solution)/shard_map/ppermute | solution.py:378
  126.5 8.0 %collective-permute-start.1 = (f32[16,208,128]{2,1,0:T(8,128)S(1)}, f32[16,208,128]{2,1,0:T(8,128)S(1)}, u32[]{:S(2)}, u32[]{:S(2)}) collective-permute-start(f32[16,208,128]{2,1,0:T(8,128)S(1)} %all_to_all.28.mine), channel_id=1, source_target_pairs={{0,1},{1,0},{2,3},{3,2},{4,5},{5,4},{6,7},{7,6},{8,9},{9,8},{10,11... | collective-permute-start | bytes 5111816 | tf_op jit(solution)/shard_map/ppermute | solution.py:396
  131.3 3.2 %collective-permute-start.2 = (f32[8,128]{1,0:T(8,128)S(1)}, f32[8,128]{1,0:T(8,128)S(1)}, u32[]{:S(2)}, u32[]{:S(2)}) collective-permute-start(f32[8,128]{1,0:T(8,128)S(1)} %get-tuple-element.25.gain_mine), channel_id=1, source_target_pairs={{0,1},{1,0},{2,3},{3,2},{4,5},{5,4},{6,7},{7,6},{8,9},{9,8},{10,11... | collective-permute-start | bytes 12296 | tf_op jit(solution)/shard_map/ppermute | solution.py:392

commit v2 on v1

v2 whole, which is shorter than its diff:
```python
import functools

import jax
import jax.numpy as jnp
from jax import lax
from jax.experimental import pallas as pl
from jax.experimental.pallas import tpu as pltpu
from jax.sharding import Mesh, PartitionSpec as P

GAP = 2
TEMPERATURE = 0.1
EPS = 1e-05
HIGHEST = lax.Precision.HIGHEST

SEGS = 16
LEN = 128
C = 512
PROJ = 128
TAPS = 3
STEP_SEGS = 4
ROWS = STEP_SEGS * LEN
STEPS = SEGS // STEP_SEGS
JOIN = 2

RANKS = 8
PEERS = 32
STACKS = 4
BLOCKS = TAPS * C // 128
HALF = BLOCKS // 2
EACH = C // PEERS
CONV_ROWS = HALF * EACH
PROJ_ROWS = C // 2 // PEERS
CHUNK = CONV_ROWS + PROJ_ROWS
GAIN_ROWS = 8
LONG = CHUNK + GAIN_ROWS

VMEM = pltpu.VMEM
SMEM = pltpu.SMEM
DMA = pltpu.SemaphoreType.DMA
IN_HBM = pl.BlockSpec(memory_space=pl.ANY)
FULL = 67043328
IN_VMEM = pl.BlockSpec(memory_space=VMEM)
IN_SMEM = pl.BlockSpec(memory_space=SMEM)


def whole(shape, space=None):
    zeros = (0,) * len(shape)
    return pl.BlockSpec(shape, lambda *_: zeros, memory_space=space)


def later(rows):
    return jnp.concatenate([rows[GAP:], jnp.zeros((GAP, rows.shape[1]), rows.dtype)], axis=0)


def earlier(rows):
    return jnp.concatenate([jnp.zeros((GAP, rows.shape[1]), rows.dtype), rows[:-GAP]], axis=0)


def unit_rows(values):
    return values * lax.rsqrt(jnp.mean(values * values, axis=-1, keepdims=True) + EPS)


def forward_kernel(
    group_hbm, segments_hbm, weight_hbm, gain_hbm, head_hbm,
    normed_hbm, slope_hbm, pooled_out, projected_out, send_out,
    group, segments, weight, gain, head, pooled, normed_out, slope_out, step_sems, out_sems, sems,
):
    cubic = 0.044715
    scale = 0.7978845608028654

    def fetch(step):
        span = pl.ds(step * STEP_SEGS, STEP_SEGS)
        return pltpu.make_async_copy(segments_hbm.at[0, span], segments.at[span], step_sems.at[step])

    def store(step):
        span = pl.ds(step * STEP_SEGS, STEP_SEGS)
        return (
            pltpu.make_async_copy(normed_out.at[span], normed_hbm.at[span], out_sems.at[0, step]),
            pltpu.make_async_copy(slope_out.at[span], slope_hbm.at[span], out_sems.at[1, step]),
        )

    gain_copy = pltpu.make_async_copy(gain_hbm, gain, sems.at[0])
    weight_copy = pltpu.make_async_copy(weight_hbm, weight, sems.at[1])
    head_copy = pltpu.make_async_copy(head_hbm, head, sems.at[2])
    group_copy = pltpu.make_async_copy(group_hbm, group, sems.at[3])
    gain_copy.start()
    fetch(0).start()
    weight_copy.start()
    for step in range(1, STEPS):
        fetch(step).start()
    head_copy.start()
    group_copy.start()
    gain_copy.wait()

    def one_step(step, carry):
        fetch(step).wait()

        @pl.when(step == 0)
        def _():
            weight_copy.wait()

        for first in range(0, STEP_SEGS, JOIN):
            wide = []
            for index in range(first, first + JOIN):
                segment = step * STEP_SEGS + index
                normed = (unit_rows(segments[segment].astype(jnp.float32)) * gain[...]).astype(jnp.bfloat16)
                normed_out[segment] = normed
                wide.append(jnp.concatenate([earlier(normed), normed, later(normed)], axis=1))
            joined = jnp.dot(jnp.concatenate(wide, axis=0), weight[...], preferred_element_type=jnp.float32)
            for index in range(first, first + JOIN):
                segment = step * STEP_SEGS + index
                inputs = segments[segment].astype(jnp.float32)
                conv = joined[(index - first) * LEN : (index - first + 1) * LEN]
                square = conv * conv
                bent = jnp.tanh(conv * (scale + (scale * cubic) * square))
                half = 0.5 + 0.5 * bent
                hidden = inputs + conv * half
                slope_out[segment] = half + (0.5 * conv) * (1.0 - bent * bent) * (
                    scale + (3.0 * scale * cubic) * square
                )
                pooled[pl.ds(segment, 1), :] = jnp.sum(hidden, axis=0, keepdims=True) * (1.0 / LEN)
        for copy in store(step):
            copy.start()
        return carry

    lax.fori_loop(0, STEPS, one_step, 0)
    head_copy.wait()
    group_copy.wait()
    rounded = pooled[...].astype(jnp.bfloat16)
    pooled_out[...] = rounded
    projected = jnp.dot(rounded, head[...], preferred_element_type=jnp.float32)
    projected_out[...] = projected
    embedding = unit_rows(projected) * PROJ ** (-0.5)
    lane = lax.broadcasted_iota(jnp.int32, (8, 128), 1) & (SEGS - 1)
    groups = jnp.zeros((8, 128), jnp.int32)
    for index in range(SEGS):
        groups = jnp.where(lane == index, group[0, index], groups)
    groups = groups.astype(jnp.float32)
    for rank in range(RANKS):
        send_out[rank, 0:SEGS, :] = embedding
        send_out[rank, SEGS:, :] = groups
    for step in range(STEPS):
        for copy in store(step):
            copy.wait()


def forward(group, segments, weight, gain, head):
    f32 = jnp.float32
    bf16 = jnp.bfloat16
    return pl.pallas_call(
        forward_kernel,
        in_specs=[IN_HBM] * 5,
        out_specs=[IN_HBM] * 2 + [IN_VMEM] * 3,
        out_shape=[
            jax.ShapeDtypeStruct((SEGS, LEN, C), bf16),
            jax.ShapeDtypeStruct((SEGS, LEN, C), f32),
            jax.ShapeDtypeStruct((SEGS, C), bf16),
            jax.ShapeDtypeStruct((SEGS, PROJ), f32),
            jax.ShapeDtypeStruct((RANKS, SEGS + 8, PROJ), f32),
        ],
        scratch_shapes=[
            SMEM((1, SEGS), jnp.int32),
            VMEM((SEGS, LEN, C), bf16),
            VMEM((TAPS * C, C), bf16),
            VMEM((1, C), f32),
            VMEM((C, PROJ), bf16),
            VMEM((SEGS, C), f32),
            VMEM((SEGS, LEN, C), bf16),
            VMEM((SEGS, LEN, C), f32),
            DMA((STEPS,)),
            DMA((2, STEPS)),
            DMA((4,)),
        ],
        compiler_params=pltpu.CompilerParams(vmem_limit_bytes=FULL),
        cost_estimate=pl.CostEstimate(flops=2 * SEGS * LEN * TAPS * C * C, bytes_accessed=10 << 20, transcendentals=SEGS * LEN * C),
        name="forward",
    )(group, segments, weight.reshape(TAPS * C, C), gain, head)


def loss_gradient(positive, gathered, projected, pooled, head, partner, place):
    embeddings = gathered[:, 0:SEGS, :].reshape(RANKS * SEGS, PROJ)
    own = unit_rows(projected[...]) * PROJ ** (-0.5)
    count = RANKS * SEGS
    nt = (((1,), (1,)), ((), ()))
    lane = lax.broadcasted_iota(jnp.int32, (8, 128), 1)
    groups = jnp.zeros((8, 128), jnp.float32)
    for rank in range(RANKS):
        groups = jnp.where(lane >> 4 == rank, gathered[rank, SEGS:, :], groups)
    by_column = jnp.broadcast_to(groups[0:1], (count, count))
    by_row = by_column.T
    row = lax.broadcasted_iota(jnp.int32, (count, count), 0)
    column = lax.broadcasted_iota(jnp.int32, (count, count), 1)
    same = (by_row == by_column) & (row != column)
    scores = lax.dot_general(
        embeddings, embeddings, nt, precision=HIGHEST, preferred_element_type=jnp.float32
    ) / TEMPERATURE
    column_total = jnp.log(jnp.sum(jnp.where(same, jnp.exp(scores), 0.0), axis=0, keepdims=True))

    own_scores = lax.dot_general(
        own, embeddings, nt, precision=HIGHEST, preferred_element_type=jnp.float32
    ) / TEMPERATURE
    own_row = lax.broadcasted_iota(jnp.int32, (SEGS, count), 0) + place * SEGS
    own_column = lax.broadcasted_iota(jnp.int32, (SEGS, count), 1)
    own_group = jnp.sum(jnp.where(own_row == own_column, groups[0:1], 0.0), axis=1, keepdims=True)
    own_same = (own_group == groups[0:1]) & (own_row != own_column)
    own_total = jnp.log(jnp.sum(jnp.where(own_same, jnp.exp(own_scores), 0.0), axis=1, keepdims=True))
    both = jnp.where(own_same, jnp.exp(own_scores - own_total) + jnp.exp(own_scores - column_total), 0.0)
    pulled = jnp.dot(both, embeddings, precision=HIGHEST, preferred_element_type=jnp.float32)
    for index in range(SEGS):
        where = positive[0, index]
        partner[index : index + 1, :] = gathered[where >> 4, pl.ds(where & (SEGS - 1), 1), :]
    factor = (count * 32) ** (-0.5) / TEMPERATURE
    embed_grad = factor * (pulled - 2.0 * partner[...])

    values = projected[...]
    inverse = lax.rsqrt(jnp.mean(values * values, axis=-1, keepdims=True) + EPS)
    outer = embed_grad * PROJ ** (-0.5)
    dotted = jnp.mean(values * outer, axis=-1, keepdims=True)
    projected_grad = inverse * outer - values * (inverse * inverse * inverse * dotted)
    derivative = lax.dot_general(
        pooled[...].astype(jnp.float32),
        projected_grad,
        (((0,), (0,)), ((), ())),
        precision=HIGHEST,
        preferred_element_type=jnp.float32,
    )
    hidden_grad = lax.dot_general(
        projected_grad, head[...].astype(jnp.float32), nt, precision=HIGHEST, preferred_element_type=jnp.float32
    ) * (1.0 / LEN)
    return derivative, hidden_grad


def weight_kernel(
    places, positive_hbm, gathered, projected, pooled, head_hbm, normed_hbm, slope_hbm,
    grad_hbm, keep_out, send_out,
    total, hidden_grad, derivative, partner, positive, head, normed, slope, grad_out, sems, step_sems,
):
    def fetch(step):
        span = pl.ds(step * STEP_SEGS, STEP_SEGS)
        return (
            pltpu.make_async_copy(slope_hbm.at[span], slope.at[span], step_sems.at[0, step]),
            pltpu.make_async_copy(normed_hbm.at[span], normed.at[span], step_sems.at[1, step]),
        )

    def store(step):
        span = pl.ds(step * STEP_SEGS, STEP_SEGS)
        return pltpu.make_async_copy(grad_out.at[span], grad_hbm.at[span], step_sems.at[2, step])

    head_copy = pltpu.make_async_copy(head_hbm, head, sems.at[0])
    positive_copy = pltpu.make_async_copy(positive_hbm, positive, sems.at[1])
    head_copy.start()
    positive_copy.start()
    for step in range(STEPS):
        for copy in fetch(step):
            copy.start()
    head_copy.wait()
    positive_copy.wait()
    derivative[...], hidden_grad[...] = loss_gradient(
        positive, gathered, projected, pooled, head, partner, places[0]
    )
    total[...] = jnp.zeros_like(total)

    def one_step(step, carry):
        for copy in fetch(step):
            copy.wait()
        sides = []
        for index in range(STEP_SEGS):
            segment = step * STEP_SEGS + index
            grad = (hidden_grad[pl.ds(segment, 1), :] * slope[segment]).astype(jnp.bfloat16)
            grad_out[segment] = grad
            sides.append(jnp.concatenate([later(grad), grad, earlier(grad)], axis=1))
        rows = normed[pl.ds(step * STEP_SEGS, STEP_SEGS)].reshape(ROWS, C)
        product = lax.dot_general(
            rows, jnp.concatenate(sides, axis=0), (((0,), (0,)), ((), ())), preferred_element_type=jnp.float32
        )
        for block in range(BLOCKS):
            total[block] += product[:, block * 128 : (block + 1) * 128]
        store(step).start()
        return carry

    lax.fori_loop(0, STEPS, one_step, 0)
    core = places[1]
    for target, which in ((keep_out, core), (send_out, 1 - core)):
        for peer in range(PEERS):
            for block in range(HALF):
                target[peer, block * EACH : (block + 1) * EACH, :] = total[
                    which * HALF + block, peer * EACH : (peer + 1) * EACH, :
                ]
            target[peer, CONV_ROWS:, :] = derivative[
                pl.ds(pl.multiple_of(which * (C // 2) + peer * PROJ_ROWS, PROJ_ROWS), PROJ_ROWS), :
            ]
    for step in range(STEPS):
        store(step).wait()


def weight_gradient(places, positive, gathered, projected, pooled, head, normed, slope):
    f32 = jnp.float32
    bf16 = jnp.bfloat16
    return pl.pallas_call(
        weight_kernel,
        in_specs=[IN_SMEM, IN_HBM, IN_VMEM, IN_VMEM, IN_VMEM, IN_HBM, IN_HBM, IN_HBM],
        out_specs=[IN_HBM] + [IN_VMEM] * 2,
        out_shape=[
            jax.ShapeDtypeStruct((SEGS, LEN, C), bf16),
            jax.ShapeDtypeStruct((PEERS, CHUNK, 128), f32),
            jax.ShapeDtypeStruct((PEERS, CHUNK, 128), f32),
        ],
        scratch_shapes=[
            VMEM((BLOCKS, C, 128), f32),
            VMEM((SEGS, C), f32),
            VMEM((C, PROJ), f32),
            VMEM((SEGS, PROJ), f32),
            SMEM((1, SEGS), jnp.int32),
            VMEM((C, PROJ), bf16),
            VMEM((SEGS, LEN, C), bf16),
            VMEM((SEGS, LEN, C), f32),
            VMEM((SEGS, LEN, C), bf16),
            DMA((2,)),
            DMA((3, STEPS)),
        ],
        compiler_params=pltpu.CompilerParams(vmem_limit_bytes=FULL),
        cost_estimate=pl.CostEstimate(flops=2 * SEGS * LEN * TAPS * C * C, bytes_accessed=12 << 20, transcendentals=1 << 16),
        name="weight_gradient",
    )(places, positive, gathered, projected, pooled, head, normed, slope)


def gain_kernel(grad, segments, weight, out, total, wide):
    step = pl.program_id(0)

    @pl.when(step == 0)
    def _():
        total[...] = jnp.zeros_like(total)
        for tap in range(TAPS):
            wide[:, tap * C : (tap + 1) * C] = weight[tap]

    for first in range(0, STEP_SEGS, JOIN):
        sides = []
        for index in range(first, first + JOIN):
            middle = grad[index]
            sides.append(jnp.concatenate([later(middle), middle, earlier(middle)], axis=1))
        joined = lax.dot_general(
            jnp.concatenate(sides, axis=0), wide[...], (((1,), (1,)), ((), ())), preferred_element_type=jnp.float32
        )
        for index in range(first, first + JOIN):
            product = joined[(index - first) * LEN : (index - first + 1) * LEN] * unit_rows(
                segments[0, index].astype(jnp.float32)
            )
            total[...] += jnp.sum(product.reshape(LEN // 8, 8, C), axis=0)

    @pl.when(step == STEPS - 1)
    def _():
        summed = jnp.sum(total[...], axis=0, keepdims=True)
        for block in range(GAIN_ROWS):
            at = block % (C // 128)
            out[block : block + 1, :] = summed[:, at * 128 : (at + 1) * 128]


def gain_gradient(grad, segments, weight):
    f32 = jnp.float32
    return pl.pallas_call(
        gain_kernel,
        grid=(STEPS,),
        in_specs=[
            pl.BlockSpec((STEP_SEGS, LEN, C), lambda i: (i, 0, 0)),
            pl.BlockSpec((1, STEP_SEGS, LEN, C), lambda i: (0, i, 0, 0)),
            whole((TAPS, C, C)),
        ],
        out_specs=whole((GAIN_ROWS, 128)),
        out_shape=jax.ShapeDtypeStruct((GAIN_ROWS, 128), f32),
        scratch_shapes=[VMEM((8, C), f32), VMEM((C, TAPS * C), jnp.bfloat16)],
        compiler_params=pltpu.CompilerParams(vmem_limit_bytes=32 << 20),
        cost_estimate=pl.CostEstimate(flops=2 * SEGS * LEN * TAPS * C * C, bytes_accessed=6 << 20, transcendentals=0),
        name="gain_gradient",
    )(grad, segments, weight)


def small_call(body, out_shape, name, *args):
    return pl.pallas_call(
        body,
        out_shape=out_shape,
        compiler_params=pltpu.CompilerParams(vmem_limit_bytes=24 << 20),
        cost_estimate=pl.CostEstimate(flops=1 << 20, bytes_accessed=4 << 20, transcendentals=0),
        name=name,
    )(*args)


def peer_sum_kernel(received, gain, out):
    summed = received[0]
    for source in range(1, PEERS):
        summed = summed + received[source]
    for stack in range(STACKS):
        out[stack, 0:CHUNK, :] = summed
        out[stack, CHUNK:, :] = gain[...]


def stack_sum_kernel(received, out):
    summed = received[0]
    for source in range(1, STACKS):
        summed = summed + received[source]
    for peer in range(PEERS):
        out[peer] = summed


def place_kernel(flip, places, rows, *refs):
    gain_before = refs[0] if flip else None
    conv_hbm, head_hbm, gain_out, sems = refs[-4:]
    wide = C // 128
    half = 1 - places[1] if flip else places[1]
    copies = []
    for block in range(HALF):
        at = half * HALF + block
        tap = at >> 2
        lanes = pl.ds(pl.multiple_of((at & 3) * 128, 128), 128)
        source = rows.at[:, pl.ds(block * EACH, EACH), :]
        copies.append(pltpu.make_async_copy(source, conv_hbm.at[tap, :, :, lanes], sems.at[block]))
    source = rows.at[:, pl.ds(CONV_ROWS, PROJ_ROWS), :]
    copies.append(pltpu.make_async_copy(source, head_hbm.at[half], sems.at[HALF]))
    for copy in copies:
        copy.start()
    summed = rows[0, CHUNK:, :]
    for peer in range(1, PEERS):
        summed = summed + rows[peer, CHUNK:, :]
    if flip:
        gain_out[...] = (summed + gain_before[...])[0:wide, :]
    else:
        gain_out[...] = summed
    for copy in copies:
        copy.wait()


def place(flip, places, rows, before=None):
    f32 = jnp.float32
    return pl.pallas_call(
        functools.partial(place_kernel, flip),
        in_specs=[IN_SMEM, IN_VMEM] + ([IN_VMEM, IN_HBM, IN_HBM] if flip else []),
        out_specs=[IN_HBM, IN_HBM, IN_VMEM],
        out_shape=(
            jax.ShapeDtypeStruct((TAPS, PEERS, EACH, C), f32),
            jax.ShapeDtypeStruct((2, PEERS, PROJ_ROWS, PROJ), f32),
            jax.ShapeDtypeStruct((C // 128 if flip else GAIN_ROWS, 128), f32),
        ),
        scratch_shapes=[DMA((HALF + 1,))],
        input_output_aliases={3: 0, 4: 1} if flip else {},
        compiler_params=pltpu.CompilerParams(vmem_limit_bytes=24 << 20),
        cost_estimate=pl.CostEstimate(flops=1 << 20, bytes_accessed=4 << 20, transcendentals=0),
        name="place_other" if flip else "place_mine",
    )(places, rows, *((before[2], before[0], before[1]) if flip else ()))


def body(segments, conv_weight, gain, head, group, positive):
    f32 = jnp.float32
    peers = ("x", "yh", "zl", "yl")
    swap = [(0, 1), (1, 0)]
    places = jnp.stack([lax.axis_index(("x", "yh")), lax.axis_index("core")]).astype(jnp.int32)
    normed, slope, pooled, projected, send = forward(group, segments, conv_weight, gain.reshape(1, C), head)
    gathered = lax.all_to_all(send, ("x", "yh"), 0, 0)
    grad, keep, give = weight_gradient(places, positive, gathered, projected, pooled, head, normed, slope)
    received = lax.ppermute(give, "core", swap)
    paired = keep + received
    across = lax.all_to_all(paired, peers, 0, 0)
    gain_part = gain_gradient(grad, segments, conv_weight)
    summed = small_call(
        peer_sum_kernel, jax.ShapeDtypeStruct((STACKS, LONG, 128), f32), "peer_sum", across, gain_part
    )
    along = lax.all_to_all(summed, "zh", 0, 0)
    spread = small_call(stack_sum_kernel, jax.ShapeDtypeStruct((PEERS, LONG, 128), f32), "stack_sum", along)
    mine = lax.all_to_all(spread, peers, 0, 0)
    other = lax.ppermute(mine, "core", swap)
    conv_grad, head_grad, gain_grad = place(True, places, other, place(False, places, mine))
    return conv_grad.reshape(TAPS, C, C), gain_grad.reshape(C), head_grad.reshape(C, PROJ)


def solution(mesh):
    fine = Mesh(mesh.devices.reshape(4, 2, 4, 2, 2, 2), ("x", "yh", "zh", "zl", "yl", "core"))
    row, grp = ("x", "yh"), ("zh", "zl", "yl", "core")
    placed = (P(grp, row, None, None), P(), P(), P(), P(grp, row), P(grp, row))
    return jax.shard_map(body, mesh=fine, in_specs=placed, out_specs=(P(), P(), P()), check_vma=False)
```

time: 137 us -> 129 us (0.942)
  blocking collectives: 77 us -> 45.2 us
  waiting for transfers between devices: 9.81 us -> 27.9 us
  starting transfers between devices: 14.4 us -> 18.5 us
  local copies, waits for them, and re-layouts: 6.57 us -> 3.18 us
  other arithmetic: 0.07 us -> 3.44 us
    all_to_all x4 -> x2, blocking collectives: 77 us -> 45.2 us  [the longest x1 28.7 us: body(): mine = lax.all_to_all(spread, peers, 0, 0)]
    all_to_all x0 -> x1, waiting for transfers between devices: none -> 16.7 us  [body(): across = lax.all_to_all(paired, peers, 0, 0)]
    all_to_all x0 -> x1, starting transfers between devices: none -> 4.45 us  [body(): across = lax.all_to_all(paired, peers, 0, 0)]
    ppermute x1, waiting for transfers between devices: 0.01 us -> 3.43 us  [body(): received = lax.ppermute(give, 'core', swap)]
    unnamed x20 -> x8, local copies, waits for them, and re-layouts: 6.57 us -> 3.18 us
    ppermute x1 -> x0, waiting for transfers between devices: 3.23 us -> none  [body(): gain_other = lax.ppermute(gain_mine, 'core', swap)]
    add x0 -> x1, other arithmetic: none -> 2.86 us  [body(): paired = keep + received]
    ppermute x1, waiting for transfers between devices: 0.01 us -> 1.62 us  [body(): other = lax.ppermute(mine, 'core', swap)]
  transfers between devices with their start and end apart: 4 -> 4, of which waited for: 2 -> 4; matrix products, arithmetic and copies ran while one was open for 0% -> 0% of each run, Pallas kernels for 6% -> 5%
where the time goes in v2:
time: 129 us
  blocking collectives  45.2 us (35%)
  Pallas kernels  29.6 us (23%)
  waiting for transfers between devices  27.9 us (22%)
  starting transfers between devices  18.5 us (14%)
  other arithmetic  3.44 us (3%)
  local copies, waits for them, and re-layouts  3.18 us (2%)
    all_to_all x1, blocking collectives, body(): mine = lax.all_to_all(spread, peers, 0, 0)  28.7 us
    all_to_all x1, waiting for transfers between devices, body(): across = lax.all_to_all(paired, peers, 0, 0)  16.7 us
    all_to_all x1, blocking collectives, body(): along = lax.all_to_all(summed, 'zh', 0, 0)  16.5 us
    pallas_call x1, Pallas kernels, weight_gradient(): pl.pallas_call(weight_kernel, in_specs=[IN_SMEM, IN_HBM, IN_VMEM, IN_VMEM...  11 us
    pallas_call x1, Pallas kernels, forward(): pl.pallas_call(forward_kernel, in_specs=[IN_HBM] * 5, out_specs=[IN_HBM]...  9.99 us
    all_to_all x1, starting transfers between devices, body(): gathered = lax.all_to_all(send, ('x', 'yh'), 0, 0)  7.47 us
    all_to_all x1, waiting for transfers between devices, body(): gathered = lax.all_to_all(send, ('x', 'yh'), 0, 0)  6.18 us
    all_to_all x1, starting transfers between devices, body(): across = lax.all_to_all(paired, peers, 0, 0)  4.45 us
  transfers between devices with their start and end apart: 4, of which 4 were waited for; matrix products, arithmetic and copies ran while one was open for 0% of the time, Pallas kernels for 5%

profile of v2, /device:TPU:1, one launch (start us, length us, event | category | flops | bytes accessed | tf_op | source)
XLA Modules:
  0.0 128.5 jit_solution(151632980410638455)
XLA Ops:
  0.6 10.0 %forward.1 = (bf16[16,128,512]{2,1,0:T(8,128)(2,1)}, f32[16,128,512]{2,1,0:T(8,128)}, bf16[16,512]{1,0:T(8,128)(2,1)}, f32[16,128]{1,0:T(8,128)}, f32[8,24,128]{2,1,0:T(8,128)}) custom-call(s32[1,16]{1,0:T(1,128)} %group_hbm.1, bf16[1,16,128,512]{3,2,1,0:T(8,128)(2,1)} %segments.1, bf16[1536,512]{1,0:T(8,128)(2,1)} %bitcast.7, f32[1,512]{1,0:T(1,128)} %bitcast.10, ...), custom_call_target="tpu_custom_call" | custom-call | flops 3221225472 | bytes 10485760 | tf_op jit(solution)/shard_map/forward/pallas_call | solution.py:150
  10.6 7.5 %all-to-all-start = ((f32[8,24,128]{2,1,0:T(8,128)}), f32[8,24,128]{2,1,0:T(8,128)}, u32[]{:S(2)}, u32[]{:S(2)}) async-start(f32[8,24,128]{2,1,0:T(8,128)} %get-tuple-element.17), calls=%async_computation | async-start | bytes 196608 | tf_op jit(solution)/shard_map/all_to_all | solution.py:456
  18.1 0.6 pad_add_fusion.places
  18.7 6.2 %all-to-all-done.gathered = f32[8,24,128]{2,1,0:T(8,128)} async-done(((f32[8,24,128]{2,1,0:T(8,128)}), f32[8,24,128]{2,1,0:T(8,128)}, u32[]{:S(2)}, u32[]{:S(2)}) %all-to-all-start) | async-done | bytes 98336 | tf_op jit(solution)/shard_map/all_to_all | solution.py:456
  24.9 11.0 %weight_gradient.1 = (bf16[16,128,512]{2,1,0:T(8,128)(2,1)}, f32[32,104,128]{2,1,0:T(8,128)}, f32[32,104,128]{2,1,0:T(8,128)}) custom-call(s32[2]{0:T(128)} %pad_add_fusion.places, s32[1,16]{1,0:T(1,128)} %positive_hbm.1, f32[8,24,128]{2,1,0:T(8,128)} %all-to-all-done.gathered, f32[16,128]{1,0:T(8,128)} %get-tuple-element.18.projected, ...), custom_call_target="tpu_custom_call" | custom-call | flops 3221225472 | bytes 12582912 | tf_op jit(solution)/shard_map/weight_gradient/pallas_call | solution.py:299
  35.9 2.2 %collective-permute-start = (f32[32,104,128]{2,1,0:T(8,128)}, f32[32,104,128]{2,1,0:T(8,128)S(1)}, u32[]{:S(2)}, u32[]{:S(2)}) collective-permute-start(f32[32,104,128]{2,1,0:T(8,128)} %get-tuple-element.23), channel_id=1, source_target_pairs={{0,1},{1,0},{2,3},{3,2},{4,5},{5,4},{6,7},{7,6},{8,9},{9,8},{10,11... | collective-permute-start | bytes 5111816 | tf_op jit(solution)/shard_map/ppermute | solution.py:458
  38.1 3.4 %collective-permute-done = f32[32,104,128]{2,1,0:T(8,128)S(1)} collective-permute-done((f32[32,104,128]{2,1,0:T(8,128)}, f32[32,104,128]{2,1,0:T(8,128)S(1)}, u32[]{:S(2)}, u32[]{:S(2)}) %collective-permute-start) | collective-permute-done | bytes 1703968 | tf_op jit(solution)/shard_map/ppermute | solution.py:458
  41.5 2.9 %add.7 = f32[32,104,128]{2,1,0:T(8,128)} add(f32[32,104,128]{2,1,0:T(8,128)} %get-tuple-element.22, f32[32,104,128]{2,1,0:T(8,128)S(1)} %collective-permute-done) | non-fusion elementwise | flops 425984 | bytes 5111808 | tf_op jit(solution)/shard_map/add | solution.py:459
  44.4 0.0 copy-start.2
  44.4 4.4 %all-to-all-start.1 = ((f32[32,104,128]{2,1,0:T(8,128)}), f32[32,104,128]{2,1,0:T(8,128)S(1)}, u32[]{:S(2)}, u32[]{:S(2)}) async-start(f32[32,104,128]{2,1,0:T(8,128)} %add.7), calls=%async_computation.1 | async-start | bytes 3407872 | tf_op jit(solution)/shard_map/all_to_all | solution.py:460
  48.8 0.0 copy-done.2
  48.8 0.0 copy-start.1
  48.9 1.6 %copy-done.1 = bf16[1,16,128,512]{3,2,1,0:T(8,128)(2,1)S(1)} copy-done((bf16[1,16,128,512]{3,2,1,0:T(8,128)(2,1)S(1)}, bf16[1,16,128,512]{3,2,1,0:T(8,128)(2,1)}, u32[]{:S(2)}) %copy-start.1) | copy-done | bytes 2097176
  50.4 0.0 copy-start.3
  50.4 1.6 %copy-done.3 = bf16[16,128,512]{2,1,0:T(8,128)(2,1)S(1)} copy-done((bf16[16,128,512]{2,1,0:T(8,128)(2,1)S(1)}, bf16[16,128,512]{2,1,0:T(8,128)(2,1)}, u32[]{:S(2)}) %copy-start.3) | copy-done | bytes 2097176
  52.0 4.2 %gain_gradient.1.gain = f32[8,128]{1,0:T(8,128)S(1)} custom-call(bf16[16,128,512]{2,1,0:T(8,128)(2,1)S(1)} %copy-done.3, bf16[1,16,128,512]{3,2,1,0:T(8,128)(2,1)S(1)} %copy-done.1, bf16[3,512,512]{2,1,0:T(8,128)(2,1)S(1)} %copy-done.2), custom_call_target="tpu_custom_call" | custom-call | flops 3221225472 | bytes 6291456 | tf_op jit(solution)/shard_map/gain_gradient/pallas_call | solution.py:360
  56.3 16.7 %all-to-all-done.1.received = f32[32,104,128]{2,1,0:T(8,128)S(1)} async-done(((f32[32,104,128]{2,1,0:T(8,128)}), f32[32,104,128]{2,1,0:T(8,128)S(1)}, u32[]{:S(2)}, u32[]{:S(2)}) %all-to-all-start.1) | async-done | bytes 1703968 | tf_op jit(solution)/shard_map/all_to_all | solution.py:460
  72.9 0.1 peer_sum.1
  73.0 16.5 %all_to_all.20.received = f32[4,112,128]{2,1,0:T(8,128)S(1)} all-to-all(f32[4,112,128]{2,1,0:T(8,128)S(1)} %peer_sum.1), channel_id=1, replica_groups=mesh['x'=4,'yh'=2,'zh'=4,'zl'=2,'yl'=2,'core'=2] {'zh'}, dimensions={0} | all-to-all | bytes 458752 | tf_op jit(solution)/shard_map/all_to_all | solution.py:465
  89.5 0.1 stack_sum.1
  89.6 0.0 copy-start
  89.6 28.7 %all_to_all.21.rows = f32[32,112,128]{2,1,0:T(8,128)S(1)} all-to-all(f32[32,112,128]{2,1,0:T(8,128)S(1)} %stack_sum.1), channel_id=1, replica_groups=mesh['x'=4,'yh'=2,'zh'=4,'zl'=2,'yl'=2,'core'=2] {'x','yh','zl','yl'}, dimensions={0} | all-to-all | bytes 3670016 | tf_op jit(solution)/shard_map/all_to_all | solution.py:467
  118.4 4.4 %collective-permute-start.1 = (f32[32,112,128]{2,1,0:T(8,128)S(1)}, f32[32,112,128]{2,1,0:T(8,128)S(1)}, u32[]{:S(2)}, u32[]{:S(2)}) collective-permute-start(f32[32,112,128]{2,1,0:T(8,128)S(1)} %all_to_all.21.rows), channel_id=1, source_target_pairs={{0,1},{1,0},{2,3},{3,2},{4,5},{5,4},{6,7},{7,6},{8,9},{9,8},{10,11... | collective-permute-start | bytes 5505032 | tf_op jit(solution)/shard_map/ppermute | solution.py:468
  122.8 0.0 copy-done
  122.8 1.8 %place_mine.1 = (f32[3,32,16,512]{3,2,1,0:T(8,128)}, f32[2,32,8,128]{3,2,1,0:T(8,128)}, f32[8,128]{1,0:T(8,128)S(1)}) custom-call(s32[2]{0:T(128)S(1)} %copy-done, f32[32,112,128]{2,1,0:T(8,128)S(1)} %all_to_all.21.rows), custom_call_target="tpu_custom_call" | custom-call | flops 1048576 | bytes 4194304 | tf_op jit(solution)/shard_map/place_mine/pallas_call | solution.py:433
  124.6 1.6 %collective-permute-done.1.rows = f32[32,112,128]{2,1,0:T(8,128)S(1)} collective-permute-done((f32[32,112,128]{2,1,0:T(8,128)S(1)}, f32[32,112,128]{2,1,0:T(8,128)S(1)}, u32[]{:S(2)}, u32[]{:S(2)}) %collective-permute-start.1) | collective-permute-done | bytes 1835040 | tf_op jit(solution)/shard_map/ppermute | solution.py:468
  126.2 2.4 %place_other.1 = (f32[3,32,16,512]{3,2,1,0:T(8,128)}, f32[2,32,8,128]{3,2,1,0:T(8,128)}, f32[4,128]{1,0:T(4,128)}) custom-call(s32[2]{0:T(128)S(1)} %copy-done, f32[32,112,128]{2,1,0:T(8,128)S(1)} %collective-permute-done.1.rows, f32[8,128]{1,0:T(8,128)S(1)} %get-tuple-element.25.refs_0_, ...), custom_call_target="tpu_custom_call", output_to_operand_aliasing={{0}: (3, {}), {1}: (4, {})} | custom-call | flops 1048576 | bytes 4194304 | tf_op jit(solution)/shard_map/place_other/pallas_call | solution.py:433
Async XLA Ops:
  10.6 14.2 %all-to-all-start = ((f32[8,24,128]{2,1,0:T(8,128)}), f32[8,24,128]{2,1,0:T(8,128)}, u32[]{:S(2)}, u32[]{:S(2)}) async-start(f32[8,24,128]{2,1,0:T(8,128)} %get-tuple-element.17), calls=%async_computation | async-start | bytes 196608 | tf_op jit(solution)/shard_map/all_to_all | solution.py:456
  35.9 5.6 %collective-permute-start = (f32[32,104,128]{2,1,0:T(8,128)}, f32[32,104,128]{2,1,0:T(8,128)S(1)}, u32[]{:S(2)}, u32[]{:S(2)}) collective-permute-start(f32[32,104,128]{2,1,0:T(8,128)} %get-tuple-element.23), channel_id=1, source_target_pairs={{0,1},{1,0},{2,3},{3,2},{4,5},{5,4},{6,7},{7,6},{8,9},{9,8},{10,11... | collective-permute-start | bytes 5111816 | tf_op jit(solution)/shard_map/ppermute | solution.py:458
  44.4 4.5 %copy-start.2 = (bf16[3,512,512]{2,1,0:T(8,128)(2,1)S(1)}, bf16[3,512,512]{2,1,0:T(8,128)(2,1)}, u32[]{:S(2)}) copy-start(bf16[3,512,512]{2,1,0:T(8,128)(2,1)} %weight.1) | copy-start | bytes 4718596
  44.4 28.6 %all-to-all-start.1 = ((f32[32,104,128]{2,1,0:T(8,128)}), f32[32,104,128]{2,1,0:T(8,128)S(1)}, u32[]{:S(2)}, u32[]{:S(2)}) async-start(f32[32,104,128]{2,1,0:T(8,128)} %add.7), calls=%async_computation.1 | async-start | bytes 3407872 | tf_op jit(solution)/shard_map/all_to_all | solution.py:460
  48.8 1.6 %copy-start.1 = (bf16[1,16,128,512]{3,2,1,0:T(8,128)(2,1)S(1)}, bf16[1,16,128,512]{3,2,1,0:T(8,128)(2,1)}, u32[]{:S(2)}) copy-start(bf16[1,16,128,512]{3,2,1,0:T(8,128)(2,1)} %segments.1) | copy-start | bytes 6291460
  50.4 1.6 %copy-start.3 = (bf16[16,128,512]{2,1,0:T(8,128)(2,1)S(1)}, bf16[16,128,512]{2,1,0:T(8,128)(2,1)}, u32[]{:S(2)}) copy-start(bf16[16,128,512]{2,1,0:T(8,128)(2,1)} %get-tuple-element.24.grad) | copy-start | bytes 6291460
  89.6 33.2 %copy-start = (s32[2]{0:T(128)S(1)}, s32[2]{0:T(128)}, u32[]{:S(2)}) copy-start(s32[2]{0:T(128)} %pad_add_fusion.places) | copy-start | bytes 28
  118.4 7.8 %collective-permute-start.1 = (f32[32,112,128]{2,1,0:T(8,128)S(1)}, f32[32,112,128]{2,1,0:T(8,128)S(1)}, u32[]{:S(2)}, u32[]{:S(2)}) collective-permute-start(f32[32,112,128]{2,1,0:T(8,128)S(1)} %all_to_all.21.rows), channel_id=1, source_target_pairs={{0,1},{1,0},{2,3},{3,2},{4,5},{5,4},{6,7},{7,6},{8,9},{9,8},{10,11... | collective-permute-start | bytes 5505032 | tf_op jit(solution)/shard_map/ppermute | solution.py:468

commit v3 on v2

--- a/solution.py
+++ b/solution.py
@@ -34,6 +34,10 @@
 GAIN_ROWS = 8
 LONG = CHUNK + GAIN_ROWS
 
+PACK_POOLED = 2 * SEGS
+PACK_HEAD = PACK_POOLED + SEGS * C // 128
+PACK = PACK_HEAD + C
+
 VMEM = pltpu.VMEM
 SMEM = pltpu.SMEM
 DMA = pltpu.SemaphoreType.DMA
@@ -61,9 +65,9 @@
 
 
 def forward_kernel(
-    group_hbm, segments_hbm, weight_hbm, gain_hbm, head_hbm,
-    normed_hbm, slope_hbm, pooled_out, projected_out, send_out,
-    group, segments, weight, gain, head, pooled, normed_out, slope_out, step_sems, out_sems, sems,
+    group_hbm, positive_hbm, segments_hbm, weight_hbm, gain_hbm, head_hbm,
+    normed_hbm, slope_hbm, pack_out, send_out,
+    group, positive, segments, weight, gain, head, pooled, normed_out, slope_out, step_sems, out_sems, sems,
 ):
     cubic = 0.044715
     scale = 0.7978845608028654
@@ -83,6 +87,7 @@
     weight_copy = pltpu.make_async_copy(weight_hbm, weight, sems.at[1])
     head_copy = pltpu.make_async_copy(head_hbm, head, sems.at[2])
     group_copy = pltpu.make_async_copy(group_hbm, group, sems.at[3])
+    positive_copy = pltpu.make_async_copy(positive_hbm, positive, sems.at[4])
     gain_copy.start()
     fetch(0).start()
     weight_copy.start()
@@ -90,6 +95,7 @@
         fetch(step).start()
     head_copy.start()
     group_copy.start()
+    positive_copy.start()
     gain_copy.wait()
 
     def one_step(step, carry):
@@ -126,10 +132,17 @@
     lax.fori_loop(0, STEPS, one_step, 0)
     head_copy.wait()
     group_copy.wait()
+    positive_copy.wait()
     rounded = pooled[...].astype(jnp.bfloat16)
-    pooled_out[...] = rounded
     projected = jnp.dot(rounded, head[...], preferred_element_type=jnp.float32)
-    projected_out[...] = projected
+    pack_out[0:SEGS, :] = projected
+    for index in range(SEGS):
+        row = jnp.full((1, PROJ), positive[0, index], jnp.int32)
+        pack_out[SEGS + index : SEGS + index + 1, :] = row.astype(jnp.float32)
+    for block in range(C // 128):
+        at = PACK_POOLED + block * SEGS
+        pack_out[at : at + SEGS, :] = rounded[:, block * 128 : (block + 1) * 128].astype(jnp.float32)
+    pack_out[PACK_HEAD:, :] = head[...].astype(jnp.float32)
     embedding = unit_rows(projected) * PROJ ** (-0.5)
     lane = lax.broadcasted_iota(jnp.int32, (8, 128), 1) & (SEGS - 1)
     groups = jnp.zeros((8, 128), jnp.int32)
@@ -144,21 +157,21 @@
             copy.wait()
 
 
-def forward(group, segments, weight, gain, head):
+def forward(group, positive, segments, weight, gain, head):
     f32 = jnp.float32
     bf16 = jnp.bfloat16
     return pl.pallas_call(
         forward_kernel,
-        in_specs=[IN_HBM] * 5,
-        out_specs=[IN_HBM] * 2 + [IN_VMEM] * 3,
+        in_specs=[IN_HBM] * 6,
+        out_specs=[IN_HBM] * 2 + [IN_VMEM] * 2,
         out_shape=[
             jax.ShapeDtypeStruct((SEGS, LEN, C), bf16),
             jax.ShapeDtypeStruct((SEGS, LEN, C), f32),
-            jax.ShapeDtypeStruct((SEGS, C), bf16),
-            jax.ShapeDtypeStruct((SEGS, PROJ), f32),
+            jax.ShapeDtypeStruct((PACK, PROJ), f32),
             jax.ShapeDtypeStruct((RANKS, SEGS + 8, PROJ), f32),
         ],
         scratch_shapes=[
+            SMEM((1, SEGS), jnp.int32),
             SMEM((1, SEGS), jnp.int32),
             VMEM((SEGS, LEN, C), bf16),
             VMEM((TAPS * C, C), bf16),
@@ -169,17 +182,21 @@
             VMEM((SEGS, LEN, C), f32),
             DMA((STEPS,)),
             DMA((2, STEPS)),
-            DMA((4,)),
+            DMA((5,)),
         ],
         compiler_params=pltpu.CompilerParams(vmem_limit_bytes=FULL),
         cost_estimate=pl.CostEstimate(flops=2 * SEGS * LEN * TAPS * C * C, bytes_accessed=10 << 20, transcendentals=SEGS * LEN * C),
         name="forward",
-    )(group, segments, weight.reshape(TAPS * C, C), gain, head)
-
-
-def loss_gradient(positive, gathered, projected, pooled, head, partner, place):
+    )(group, positive, segments, weight.reshape(TAPS * C, C), gain, head)
+
+
+def loss_gradient(gathered, pack, place):
+    projected = pack[0:SEGS, :]
+    pooled = jnp.concatenate(
+        [pack[PACK_POOLED + block * SEGS : PACK_POOLED + (block + 1) * SEGS, :] for block in range(C // 128)], axis=1
+    )
     embeddings = gathered[:, 0:SEGS, :].reshape(RANKS * SEGS, PROJ)
-    own = unit_rows(projected[...]) * PROJ ** (-0.5)
+    own = unit_rows(projected) * PROJ ** (-0.5)
     count = RANKS * SEGS
     nt = (((1,), (1,)), ((), ()))
     lane = lax.broadcasted_iota(jnp.int32, (8, 128), 1)
@@ -206,34 +223,33 @@
     own_total = jnp.log(jnp.sum(jnp.where(own_same, jnp.exp(own_scores), 0.0), axis=1, keepdims=True))
     both = jnp.where(own_same, jnp.exp(own_scores - own_total) + jnp.exp(own_scores - column_total), 0.0)
     pulled = jnp.dot(both, embeddings, precision=HIGHEST, preferred_element_type=jnp.float32)
-    for index in range(SEGS):
-        where = positive[0, index]
-        partner[index : index + 1, :] = gathered[where >> 4, pl.ds(where & (SEGS - 1), 1), :]
+    picked = (pack[SEGS : 2 * SEGS, :] == own_column.astype(jnp.float32)).astype(jnp.float32)
+    partner = jnp.dot(picked, embeddings, precision=HIGHEST, preferred_element_type=jnp.float32)
     factor = (count * 32) ** (-0.5) / TEMPERATURE
-    embed_grad = factor * (pulled - 2.0 * partner[...])
-
-    values = projected[...]
+    embed_grad = factor * (pulled - 2.0 * partner)
+
+    values = projected
     inverse = lax.rsqrt(jnp.mean(values * values, axis=-1, keepdims=True) + EPS)
     outer = embed_grad * PROJ ** (-0.5)
     dotted = jnp.mean(values * outer, axis=-1, keepdims=True)
     projected_grad = inverse * outer - values * (inverse * inverse * inverse * dotted)
     derivative = lax.dot_general(
-        pooled[...].astype(jnp.float32),
+        pooled,
         projected_grad,
         (((0,), (0,)), ((), ())),
         precision=HIGHEST,
         preferred_element_type=jnp.float32,
     )
     hidden_grad = lax.dot_general(
-        projected_grad, head[...].astype(jnp.float32), nt, precision=HIGHEST, preferred_element_type=jnp.float32
+        projected_grad, pack[PACK_HEAD:, :], nt, precision=HIGHEST, preferred_element_type=jnp.float32
     ) * (1.0 / LEN)
     return derivative, hidden_grad
 
 
 def weight_kernel(
-    places, positive_hbm, gathered, projected, pooled, head_hbm, normed_hbm, slope_hbm,
+    places, gathered, pack, normed_hbm, slope_hbm,
     grad_hbm, keep_out, send_out,
-    total, hidden_grad, derivative, partner, positive, head, normed, slope, grad_out, sems, step_sems,
+    total, hidden_grad, derivative, normed, slope, grad_out, step_sems,
 ):
     def fetch(step):
         span = pl.ds(step * STEP_SEGS, STEP_SEGS)
@@ -246,18 +262,10 @@
         span = pl.ds(step * STEP_SEGS, STEP_SEGS)
         return pltpu.make_async_copy(grad_out.at[span], grad_hbm.at[span], step_sems.at[2, step])
 
-    head_copy = pltpu.make_async_copy(head_hbm, head, sems.at[0])
-    positive_copy = pltpu.make_async_copy(positive_hbm, positive, sems.at[1])
-    head_copy.start()
-    positive_copy.start()
     for step in range(STEPS):
         for copy in fetch(step):
             copy.start()
-    head_copy.wait()
-    positive_copy.wait()
-    derivative[...], hidden_grad[...] = loss_gradient(
-        positive, gathered, projected, pooled, head, partner, places[0]
-    )
+    derivative[...], hidden_grad[...] = loss_gradient(gathered, pack, places[0])
     total[...] = jnp.zeros_like(total)
 
     def one_step(step, carry):
@@ -293,12 +301,12 @@
         store(step).wait()
 
 
-def weight_gradient(places, positive, gathered, projected, pooled, head, normed, slope):
+def weight_gradient(places, gathered, pack, normed, slope):
     f32 = jnp.float32
     bf16 = jnp.bfloat16
     return pl.pallas_call(
         weight_kernel,
-        in_specs=[IN_SMEM, IN_HBM, IN_VMEM, IN_VMEM, IN_VMEM, IN_HBM, IN_HBM, IN_HBM],
+        in_specs=[IN_SMEM, IN_VMEM, IN_VMEM, IN_HBM, IN_HBM],
         out_specs=[IN_HBM] + [IN_VMEM] * 2,
         out_shape=[
             jax.ShapeDtypeStruct((SEGS, LEN, C), bf16),
@@ -309,19 +317,15 @@
             VMEM((BLOCKS, C, 128), f32),
             VMEM((SEGS, C), f32),
             VMEM((C, PROJ), f32),
-            VMEM((SEGS, PROJ), f32),
-            SMEM((1, SEGS), jnp.int32),
-            VMEM((C, PROJ), bf16),
             VMEM((SEGS, LEN, C), bf16),
             VMEM((SEGS, LEN, C), f32),
             VMEM((SEGS, LEN, C), bf16),
-            DMA((2,)),
             DMA((3, STEPS)),
         ],
-        compiler_params=pltpu.CompilerParams(vmem_limit_bytes=FULL),
+        compiler_params=pltpu.CompilerParams(vmem_limit_bytes=48 << 20),
         cost_estimate=pl.CostEstimate(flops=2 * SEGS * LEN * TAPS * C * C, bytes_accessed=12 << 20, transcendentals=1 << 16),
         name="weight_gradient",
-    )(places, positive, gathered, projected, pooled, head, normed, slope)
+    )(places, gathered, pack, normed, slope)
 
 
 def gain_kernel(grad, segments, weight, out, total, wide):
@@ -382,6 +386,12 @@
         cost_estimate=pl.CostEstimate(flops=1 << 20, bytes_accessed=4 << 20, transcendentals=0),
         name=name,
     )(*args)
+
+
+def pair_sum_kernel(keep, received, gain, out, gain_out):
+    gain_out[...] = gain[...]
+    for peer in range(PEERS):
+        out[peer] = keep[peer] + received[peer]
 
 
 def peer_sum_kernel(received, gain, out):
@@ -452,13 +462,20 @@
     peers = ("x", "yh", "zl", "yl")
     swap = [(0, 1), (1, 0)]
     places = jnp.stack([lax.axis_index(("x", "yh")), lax.axis_index("core")]).astype(jnp.int32)
-    normed, slope, pooled, projected, send = forward(group, segments, conv_weight, gain.reshape(1, C), head)
+    normed, slope, pack, send = forward(group, positive, segments, conv_weight, gain.reshape(1, C), head)
     gathered = lax.all_to_all(send, ("x", "yh"), 0, 0)
-    grad, keep, give = weight_gradient(places, positive, gathered, projected, pooled, head, normed, slope)
+    grad, keep, give = weight_gradient(places, gathered, pack, normed, slope)
     received = lax.ppermute(give, "core", swap)
-    paired = keep + received
+    gain_part = gain_gradient(grad, segments, conv_weight)
+    paired, gain_part = small_call(
+        pair_sum_kernel,
+        (jax.ShapeDtypeStruct((PEERS, CHUNK, 128), f32), jax.ShapeDtypeStruct((GAIN_ROWS, 128), f32)),
+        "pair_sum",
+        keep,
+        received,
+        gain_part,
+    )
     across = lax.all_to_all(paired, peers, 0, 0)
-    gain_part = gain_gradient(grad, segments, conv_weight)
     summed = small_call(
         peer_sum_kernel, jax.ShapeDtypeStruct((STACKS, LONG, 128), f32), "peer_sum", across, gain_part
     )

time: 129 us -> 121 us (0.938)
  blocking collectives: 45.2 us -> 70 us
  waiting for transfers between devices: 27.9 us -> 8.21 us
  starting transfers between devices: 18.5 us -> 14.7 us
  other arithmetic: 3.44 us -> 0.07 us
  Pallas kernels: 29.6 us -> 26.4 us
  local copies, waits for them, and re-layouts: 3.18 us -> 0.97 us
    all_to_all x0 -> x1, blocking collectives: none -> 27.3 us  [body(): across = lax.all_to_all(paired, peers, 0, 0)]
    all_to_all x1 -> x0, waiting for transfers between devices: 16.7 us -> none  [body(): across = lax.all_to_all(paired, peers, 0, 0)]
    all_to_all x1 -> x0, starting transfers between devices: 4.45 us -> none  [body(): across = lax.all_to_all(paired, peers, 0, 0)]
    ppermute x1, waiting for transfers between devices: 3.43 us -> 0.01 us  [body(): received = lax.ppermute(give, 'core', swap)]
    pallas_call x2, Pallas kernels: 21 us -> 17.6 us  [the longest x1 10.1 us: forward(): pl.pallas_call(forward_kernel, in_specs=[IN_HBM] * 6, out_specs=[IN_HBM]...]
    add x1 -> x0, other arithmetic: 2.86 us -> none  [body(): paired = keep + received]
    unnamed x8 -> x6, local copies, waits for them, and re-layouts: 3.18 us -> 0.97 us
    all_to_all x1, blocking collectives: 16.5 us -> 14.8 us  [body(): along = lax.all_to_all(summed, 'zh', 0, 0)]
  transfers between devices with their start and end apart: 4 -> 3, of which waited for: 4 -> 2; matrix products, arithmetic and copies ran while one was open for 0% -> 0% of each run, Pallas kernels for 5% -> 5%
where the time goes in v3:
time: 121 us
  blocking collectives  70 us (58%)
  Pallas kernels  26.4 us (22%)
  starting transfers between devices  14.7 us (12%)
  waiting for transfers between devices  8.21 us (7%)
    all_to_all x1, blocking collectives, body(): mine = lax.all_to_all(spread, peers, 0, 0)  27.8 us
    all_to_all x1, blocking collectives, body(): across = lax.all_to_all(paired, peers, 0, 0)  27.3 us
    all_to_all x1, blocking collectives, body(): along = lax.all_to_all(summed, 'zh', 0, 0)  14.8 us
    pallas_call x1, Pallas kernels, forward(): pl.pallas_call(forward_kernel, in_specs=[IN_HBM] * 6, out_specs=[IN_HBM]...  10.1 us
    all_to_all x1, starting transfers between devices, body(): gathered = lax.all_to_all(send, ('x', 'yh'), 0, 0)  7.49 us
    pallas_call x1, Pallas kernels, weight_gradient(): pl.pallas_call(weight_kernel, in_specs=[IN_SMEM, IN_VMEM, IN_VMEM, IN_HBM...  7.47 us
    all_to_all x1, waiting for transfers between devices, body(): gathered = lax.all_to_all(send, ('x', 'yh'), 0, 0)  6.58 us
    ppermute x1, starting transfers between devices, body(): other = lax.ppermute(mine, 'core', swap)  5.04 us
  transfers between devices with their start and end apart: 3, of which 2 were waited for; matrix products, arithmetic and copies ran while one was open for 0% of the time, Pallas kernels for 5%

profile of v3, /device:TPU:1, one launch (start us, length us, event | category | flops | bytes accessed | tf_op | source)
XLA Modules:
  0.0 121.0 jit_solution(8678165501595323361)
XLA Ops:
  0.6 10.1 %forward.1 = (bf16[16,128,512]{2,1,0:T(8,128)(2,1)}, f32[16,128,512]{2,1,0:T(8,128)}, f32[608,128]{1,0:T(8,128)}, f32[8,24,128]{2,1,0:T(8,128)}) custom-call(s32[1,16]{1,0:T(1,128)} %group_hbm.1, s32[1,16]{1,0:T(1,128)} %positive_hbm.1, bf16[1,16,128,512]{3,2,1,0:T(8,128)(2,1)} %segments.1, bf16[1536,512]{1,0:T(8,128)(2,1)} %bitcast.7, f32[1,512]{1,0:T(1,128)} %bitcast.10, ...), custom_call_target="tpu_custom_call" | custom-call | flops 3221225472 | bytes 10485760 | tf_op jit(solution)/shard_map/forward/pallas_call | solution.py:163
  10.7 7.5 %all-to-all-start = ((f32[8,24,128]{2,1,0:T(8,128)}), f32[8,24,128]{2,1,0:T(8,128)S(1)}, u32[]{:S(2)}, u32[]{:S(2)}) async-start(f32[8,24,128]{2,1,0:T(8,128)} %get-tuple-element.18), calls=%async_computation | async-start | bytes 196608 | tf_op jit(solution)/shard_map/all_to_all | solution.py:466
  18.2 0.1 pad_add_fusion.places
  18.3 6.6 %all-to-all-done.gathered = f32[8,24,128]{2,1,0:T(8,128)S(1)} async-done(((f32[8,24,128]{2,1,0:T(8,128)}), f32[8,24,128]{2,1,0:T(8,128)S(1)}, u32[]{:S(2)}, u32[]{:S(2)}) %all-to-all-start) | async-done | bytes 98336 | tf_op jit(solution)/shard_map/all_to_all | solution.py:466
  24.9 0.0 copy-start.2
  24.9 1.0 copy-done.2
  25.9 0.0 copy-start
  25.9 0.0 copy-start.1
  25.9 7.5 %weight_gradient.1 = (bf16[16,128,512]{2,1,0:T(8,128)(2,1)S(1)}, f32[32,104,128]{2,1,0:T(8,128)S(1)}, f32[32,104,128]{2,1,0:T(8,128)S(1)}) custom-call(s32[2]{0:T(128)S(1)} %pad_add_fusion.places, f32[8,24,128]{2,1,0:T(8,128)S(1)} %all-to-all-done.gathered, f32[608,128]{1,0:T(8,128)S(1)} %copy-done.2, bf16[16,128,512]{2,1,0:T(8,128)(2,1)} %get-tuple-element.20.normed_hbm, ...), custom_call_target="tpu_custom_call" | custom-call | flops 3221225472 | bytes 12582912 | tf_op jit(solution)/shard_map/weight_gradient/pallas_call | solution.py:307
  33.3 2.2 %collective-permute-start = (f32[32,104,128]{2,1,0:T(8,128)S(1)}, f32[32,104,128]{2,1,0:T(8,128)S(1)}, u32[]{:S(2)}, u32[]{:S(2)}) collective-permute-start(f32[32,104,128]{2,1,0:T(8,128)S(1)} %get-tuple-element.23), channel_id=1, source_target_pairs={{0,1},{1,0},{2,3},{3,2},{4,5},{5,4},{6,7},{7,6},{8,9},{9,8},{10,11... | collective-permute-start | bytes 5111816 | tf_op jit(solution)/shard_map/ppermute | solution.py:468
  35.5 0.0 copy-done
  35.5 0.0 copy-done.1
  35.5 4.3 %gain_gradient.1.gain = f32[8,128]{1,0:T(8,128)S(1)} custom-call(bf16[16,128,512]{2,1,0:T(8,128)(2,1)S(1)} %get-tuple-element.24.grad, bf16[1,16,128,512]{3,2,1,0:T(8,128)(2,1)S(1)} %copy-done, bf16[3,512,512]{2,1,0:T(8,128)(2,1)S(1)} %copy-done.1), custom_call_target="tpu_custom_call" | custom-call | flops 3221225472 | bytes 6291456 | tf_op jit(solution)/shard_map/gain_gradient/pallas_call | solution.py:364
  39.8 0.0 collective-permute-done.received
  39.8 0.2 pair_sum.1
  40.0 27.3 %all_to_all.20.received = f32[32,104,128]{2,1,0:T(8,128)S(1)} all-to-all(f32[32,104,128]{2,1,0:T(8,128)S(1)} %get-tuple-element.25), channel_id=1, replica_groups=mesh['x'=4,'yh'=2,'zh'=4,'zl'=2,'yl'=2,'core'=2] {'x','yh','zl','yl'}, dimensions={0} | all-to-all | bytes 3407872 | tf_op jit(solution)/shard_map/all_to_all | solution.py:478
  67.4 0.1 peer_sum.1
  67.5 14.8 %all_to_all.21.received = f32[4,112,128]{2,1,0:T(8,128)S(1)} all-to-all(f32[4,112,128]{2,1,0:T(8,128)S(1)} %peer_sum.1), channel_id=1, replica_groups=mesh['x'=4,'yh'=2,'zh'=4,'zl'=2,'yl'=2,'core'=2] {'zh'}, dimensions={0} | all-to-all | bytes 458752 | tf_op jit(solution)/shard_map/all_to_all | solution.py:482
  82.3 0.1 stack_sum.1
  82.4 27.8 %all_to_all.22.rows = f32[32,112,128]{2,1,0:T(8,128)S(1)} all-to-all(f32[32,112,128]{2,1,0:T(8,128)S(1)} %stack_sum.1), channel_id=1, replica_groups=mesh['x'=4,'yh'=2,'zh'=4,'zl'=2,'yl'=2,'core'=2] {'x','yh','zl','yl'}, dimensions={0} | all-to-all | bytes 3670016 | tf_op jit(solution)/shard_map/all_to_all | solution.py:484
  110.2 5.0 %collective-permute-start.1 = (f32[32,112,128]{2,1,0:T(8,128)S(1)}, f32[32,112,128]{2,1,0:T(8,128)S(1)}, u32[]{:S(2)}, u32[]{:S(2)}) collective-permute-start(f32[32,112,128]{2,1,0:T(8,128)S(1)} %all_to_all.22.rows), channel_id=1, source_target_pairs={{0,1},{1,0},{2,3},{3,2},{4,5},{5,4},{6,7},{7,6},{8,9},{9,8},{10,11... | collective-permute-start | bytes 5505032 | tf_op jit(solution)/shard_map/ppermute | solution.py:485
  115.3 1.8 %place_mine.1 = (f32[3,32,16,512]{3,2,1,0:T(8,128)}, f32[2,32,8,128]{3,2,1,0:T(8,128)}, f32[8,128]{1,0:T(8,128)S(1)}) custom-call(s32[2]{0:T(128)S(1)} %pad_add_fusion.places, f32[32,112,128]{2,1,0:T(8,128)S(1)} %all_to_all.22.rows), custom_call_target="tpu_custom_call" | custom-call | flops 1048576 | bytes 4194304 | tf_op jit(solution)/shard_map/place_mine/pallas_call | solution.py:443
  117.1 1.6 %collective-permute-done.1.rows = f32[32,112,128]{2,1,0:T(8,128)S(1)} collective-permute-done((f32[32,112,128]{2,1,0:T(8,128)S(1)}, f32[32,112,128]{2,1,0:T(8,128)S(1)}, u32[]{:S(2)}, u32[]{:S(2)}) %collective-permute-start.1) | collective-permute-done | bytes 1835040 | tf_op jit(solution)/shard_map/ppermute | solution.py:485
  118.7 2.4 %place_other.1 = (f32[3,32,16,512]{3,2,1,0:T(8,128)}, f32[2,32,8,128]{3,2,1,0:T(8,128)}, f32[4,128]{1,0:T(4,128)}) custom-call(s32[2]{0:T(128)S(1)} %pad_add_fusion.places, f32[32,112,128]{2,1,0:T(8,128)S(1)} %collective-permute-done.1.rows, f32[8,128]{1,0:T(8,128)S(1)} %get-tuple-element.27.refs_0_, ...), custom_call_target="tpu_custom_call", output_to_operand_aliasing={{0}: (3, {}), {1}: (4, {})} | custom-call | flops 1048576 | bytes 4194304 | tf_op jit(solution)/shard_map/place_other/pallas_call | solution.py:443
Async XLA Ops:
  10.7 14.1 %all-to-all-start = ((f32[8,24,128]{2,1,0:T(8,128)}), f32[8,24,128]{2,1,0:T(8,128)S(1)}, u32[]{:S(2)}, u32[]{:S(2)}) async-start(f32[8,24,128]{2,1,0:T(8,128)} %get-tuple-element.18), calls=%async_computation | async-start | bytes 196608 | tf_op jit(solution)/shard_map/all_to_all | solution.py:466
  24.9 1.0 copy-start.2
  25.9 9.7 %copy-start = (bf16[1,16,128,512]{3,2,1,0:T(8,128)(2,1)S(1)}, bf16[1,16,128,512]{3,2,1,0:T(8,128)(2,1)}, u32[]{:S(2)}) copy-start(bf16[1,16,128,512]{3,2,1,0:T(8,128)(2,1)} %segments.1) | copy-start | bytes 6291460
  25.9 9.7 %copy-start.1 = (bf16[3,512,512]{2,1,0:T(8,128)(2,1)S(1)}, bf16[3,512,512]{2,1,0:T(8,128)(2,1)}, u32[]{:S(2)}) copy-start(bf16[3,512,512]{2,1,0:T(8,128)(2,1)} %weight.1) | copy-start | bytes 4718596
  33.3 6.5 %collective-permute-start = (f32[32,104,128]{2,1,0:T(8,128)S(1)}, f32[32,104,128]{2,1,0:T(8,128)S(1)}, u32[]{:S(2)}, u32[]{:S(2)}) collective-permute-start(f32[32,104,128]{2,1,0:T(8,128)S(1)} %get-tuple-element.23), channel_id=1, source_target_pairs={{0,1},{1,0},{2,3},{3,2},{4,5},{5,4},{6,7},{7,6},{8,9},{9,8},{10,11... | collective-permute-start | bytes 5111816 | tf_op jit(solution)/shard_map/ppermute | solution.py:468
  110.2 8.4 %collective-permute-start.1 = (f32[32,112,128]{2,1,0:T(8,128)S(1)}, f32[32,112,128]{2,1,0:T(8,128)S(1)}, u32[]{:S(2)}, u32[]{:S(2)}) collective-permute-start(f32[32,112,128]{2,1,0:T(8,128)S(1)} %all_to_all.22.rows), channel_id=1, source_target_pairs={{0,1},{1,0},{2,3},{3,2},{4,5},{5,4},{6,7},{7,6},{8,9},{9,8},{10,11... | collective-permute-start | bytes 5505032 | tf_op jit(solution)/shard_map/ppermute | solution.py:485

commit v4 on v3

--- a/solution.py
+++ b/solution.py
@@ -17,7 +17,10 @@
 C = 512
 PROJ = 128
 TAPS = 3
-STEP_SEGS = 4
+STEP_SEGS = 8
+F_STEP = 4
+F_STEPS = SEGS // F_STEP
+F_JOIN = 4
 ROWS = STEP_SEGS * LEN
 STEPS = SEGS // STEP_SEGS
 JOIN = 2
@@ -73,11 +76,11 @@
     scale = 0.7978845608028654
 
     def fetch(step):
-        span = pl.ds(step * STEP_SEGS, STEP_SEGS)
+        span = pl.ds(step * F_STEP, F_STEP)
         return pltpu.make_async_copy(segments_hbm.at[0, span], segments.at[span], step_sems.at[step])
 
     def store(step):
-        span = pl.ds(step * STEP_SEGS, STEP_SEGS)
+        span = pl.ds(step * F_STEP, F_STEP)
         return (
             pltpu.make_async_copy(normed_out.at[span], normed_hbm.at[span], out_sems.at[0, step]),
             pltpu.make_async_copy(slope_out.at[span], slope_hbm.at[span], out_sems.at[1, step]),
@@ -91,7 +94,7 @@
     gain_copy.start()
     fetch(0).start()
     weight_copy.start()
-    for step in range(1, STEPS):
+    for step in range(1, F_STEPS):
         fetch(step).start()
     head_copy.start()
     group_copy.start()
@@ -105,16 +108,16 @@
         def _():
             weight_copy.wait()
 
-        for first in range(0, STEP_SEGS, JOIN):
+        for first in range(0, F_STEP, F_JOIN):
             wide = []
-            for index in range(first, first + JOIN):
-                segment = step * STEP_SEGS + index
+            for index in range(first, first + F_JOIN):
+                segment = step * F_STEP + index
                 normed = (unit_rows(segments[segment].astype(jnp.float32)) * gain[...]).astype(jnp.bfloat16)
                 normed_out[segment] = normed
                 wide.append(jnp.concatenate([earlier(normed), normed, later(normed)], axis=1))
             joined = jnp.dot(jnp.concatenate(wide, axis=0), weight[...], preferred_element_type=jnp.float32)
-            for index in range(first, first + JOIN):
-                segment = step * STEP_SEGS + index
+            for index in range(first, first + F_JOIN):
+                segment = step * F_STEP + index
                 inputs = segments[segment].astype(jnp.float32)
                 conv = joined[(index - first) * LEN : (index - first + 1) * LEN]
                 square = conv * conv
@@ -129,7 +132,7 @@
             copy.start()
         return carry
 
-    lax.fori_loop(0, STEPS, one_step, 0)
+    lax.fori_loop(0, F_STEPS, one_step, 0)
     head_copy.wait()
     group_copy.wait()
     positive_copy.wait()
@@ -152,7 +155,7 @@
     for rank in range(RANKS):
         send_out[rank, 0:SEGS, :] = embedding
         send_out[rank, SEGS:, :] = groups
-    for step in range(STEPS):
+    for step in range(F_STEPS):
         for copy in store(step):
             copy.wait()
 
@@ -180,8 +183,8 @@
             VMEM((SEGS, C), f32),
             VMEM((SEGS, LEN, C), bf16),
             VMEM((SEGS, LEN, C), f32),
-            DMA((STEPS,)),
-            DMA((2, STEPS)),
+            DMA((F_STEPS,)),
+            DMA((2, F_STEPS)),
             DMA((5,)),
         ],
         compiler_params=pltpu.CompilerParams(vmem_limit_bytes=FULL),
@@ -398,15 +401,12 @@
     summed = received[0]
     for source in range(1, PEERS):
         summed = summed + received[source]
-    for stack in range(STACKS):
-        out[stack, 0:CHUNK, :] = summed
-        out[stack, CHUNK:, :] = gain[...]
-
-
-def stack_sum_kernel(received, out):
-    summed = received[0]
-    for source in range(1, STACKS):
-        summed = summed + received[source]
+    out[0:CHUNK, :] = summed
+    out[CHUNK:, :] = gain[...]
+
+
+def stack_sum_kernel(own, after, across, before, out):
+    summed = (own[...] + across[...]) + (after[...] + before[...])
     for peer in range(PEERS):
         out[peer] = summed
 
@@ -476,11 +476,11 @@
         gain_part,
     )
     across = lax.all_to_all(paired, peers, 0, 0)
-    summed = small_call(
-        peer_sum_kernel, jax.ShapeDtypeStruct((STACKS, LONG, 128), f32), "peer_sum", across, gain_part
+    chunk = small_call(peer_sum_kernel, jax.ShapeDtypeStruct((LONG, 128), f32), "peer_sum", across, gain_part)
+    rings = [lax.ppermute(chunk, "zh", [(i, (i + d) % STACKS) for i in range(STACKS)]) for d in (1, 2, 3)]
+    spread = small_call(
+        stack_sum_kernel, jax.ShapeDtypeStruct((PEERS, LONG, 128), f32), "stack_sum", chunk, *rings
     )
-    along = lax.all_to_all(summed, "zh", 0, 0)
-    spread = small_call(stack_sum_kernel, jax.ShapeDtypeStruct((PEERS, LONG, 128), f32), "stack_sum", along)
     mine = lax.all_to_all(spread, peers, 0, 0)
     other = lax.ppermute(mine, "core", swap)
     conv_grad, head_grad, gain_grad = place(True, places, other, place(False, places, mine))

time: 121 us -> 118 us (0.975)
  blocking collectives: 70 us -> 55 us
  starting transfers between devices: 14.7 us -> 23 us
  waiting for transfers between devices: 8.21 us -> 11.9 us
    all_to_all x1 -> x0, blocking collectives: 14.8 us -> none  [body(): along = lax.all_to_all(summed, 'zh', 0, 0)]
    ppermute x0 -> x3, starting transfers between devices: none -> 8.44 us  [body(): lax.ppermute(chunk, 'zh', [(i, (i + d) % STACKS) for i in range(STACKS)])]
    ppermute x0 -> x3, waiting for transfers between devices: none -> 3.67 us  [body(): lax.ppermute(chunk, 'zh', [(i, (i + d) % STACKS) for i in range(STACKS)])]
  transfers between devices with their start and end apart: 3 -> 6, of which waited for: 2 -> 3; matrix products, arithmetic and copies ran while one was open for 0% -> 0% of each run, Pallas kernels for 5% -> 5%
where the time goes in v4:
time: 118 us; the launch traced here: 117 us
  blocking collectives  55 us (47%)
  Pallas kernels  25.7 us (22%)
  starting transfers between devices  23 us (19%)
  waiting for transfers between devices  11.9 us (10%)
    all_to_all x1, blocking collectives, body(): mine = lax.all_to_all(spread, peers, 0, 0)  27.7 us
    all_to_all x1, blocking collectives, body(): across = lax.all_to_all(paired, peers, 0, 0)  27.3 us
    pallas_call x1, Pallas kernels, forward(): pl.pallas_call(forward_kernel, in_specs=[IN_HBM] * 6, out_specs=[IN_HBM]...  9.94 us
    ppermute x3, starting transfers between devices, body(): lax.ppermute(chunk, 'zh', [(i, (i + d) % STACKS) for i in range(STACKS)])  8.44 us
    pallas_call x1, Pallas kernels, weight_gradient(): pl.pallas_call(weight_kernel, in_specs=[IN_SMEM, IN_VMEM, IN_VMEM, IN_HBM...  7.49 us
    all_to_all x1, starting transfers between devices, body(): gathered = lax.all_to_all(send, ('x', 'yh'), 0, 0)  7.46 us
    all_to_all x1, waiting for transfers between devices, body(): gathered = lax.all_to_all(send, ('x', 'yh'), 0, 0)  6.58 us
    ppermute x1, starting transfers between devices, body(): other = lax.ppermute(mine, 'core', swap)  4.95 us
  transfers between devices with their start and end apart: 6, of which 3 were waited for; matrix products, arithmetic and copies ran while one was open for 0% of the time, Pallas kernels for 5%

profile of v4, /device:TPU:1, one launch (start us, length us, event | category | flops | bytes accessed | tf_op | source)
XLA Modules:
  0.0 117.4 jit_solution(1509500142814315420)
XLA Ops:
  0.6 9.9 %forward.1 = (bf16[16,128,512]{2,1,0:T(8,128)(2,1)}, f32[16,128,512]{2,1,0:T(8,128)}, f32[608,128]{1,0:T(8,128)}, f32[8,24,128]{2,1,0:T(8,128)}) custom-call(s32[1,16]{1,0:T(1,128)} %group_hbm.1, s32[1,16]{1,0:T(1,128)} %positive_hbm.1, bf16[1,16,128,512]{3,2,1,0:T(8,128)(2,1)} %segments.1, bf16[1536,512]{1,0:T(8,128)(2,1)} %bitcast.7, f32[1,512]{1,0:T(1,128)} %bitcast.10, ...), custom_call_target="tpu_custom_call" | custom-call | flops 3221225472 | bytes 10485760 | tf_op jit(solution)/shard_map/forward/pallas_call | solution.py:166
  10.6 7.5 %all-to-all-start = ((f32[8,24,128]{2,1,0:T(8,128)}), f32[8,24,128]{2,1,0:T(8,128)S(1)}, u32[]{:S(2)}, u32[]{:S(2)}) async-start(f32[8,24,128]{2,1,0:T(8,128)} %get-tuple-element.18), calls=%async_computation | async-start | bytes 196608 | tf_op jit(solution)/shard_map/all_to_all | solution.py:466
  18.0 0.1 pad_add_fusion.places
  18.1 6.6 %all-to-all-done.gathered = f32[8,24,128]{2,1,0:T(8,128)S(1)} async-done(((f32[8,24,128]{2,1,0:T(8,128)}), f32[8,24,128]{2,1,0:T(8,128)S(1)}, u32[]{:S(2)}, u32[]{:S(2)}) %all-to-all-start) | async-done | bytes 98336 | tf_op jit(solution)/shard_map/all_to_all | solution.py:466
  24.7 0.0 copy-start.2
  24.7 1.0 copy-done.2
  25.7 0.0 copy-start
  25.7 0.0 copy-start.1
  25.7 7.5 %weight_gradient.1 = (bf16[16,128,512]{2,1,0:T(8,128)(2,1)S(1)}, f32[32,104,128]{2,1,0:T(8,128)S(1)}, f32[32,104,128]{2,1,0:T(8,128)S(1)}) custom-call(s32[2]{0:T(128)S(1)} %pad_add_fusion.places, f32[8,24,128]{2,1,0:T(8,128)S(1)} %all-to-all-done.gathered, f32[608,128]{1,0:T(8,128)S(1)} %copy-done.2, bf16[16,128,512]{2,1,0:T(8,128)(2,1)} %get-tuple-element.20.normed_hbm, ...), custom_call_target="tpu_custom_call" | custom-call | flops 3221225472 | bytes 12582912 | tf_op jit(solution)/shard_map/weight_gradient/pallas_call | solution.py:310
  33.2 2.2 %collective-permute-start = (f32[32,104,128]{2,1,0:T(8,128)S(1)}, f32[32,104,128]{2,1,0:T(8,128)S(1)}, u32[]{:S(2)}, u32[]{:S(2)}) collective-permute-start(f32[32,104,128]{2,1,0:T(8,128)S(1)} %get-tuple-element.23), channel_id=1, source_target_pairs={{0,1},{1,0},{2,3},{3,2},{4,5},{5,4},{6,7},{7,6},{8,9},{9,8},{10,11... | collective-permute-start | bytes 5111816 | tf_op jit(solution)/shard_map/ppermute | solution.py:468
  35.3 0.0 copy-done
  35.3 0.0 copy-done.1
  35.4 3.8 %gain_gradient.1.gain = f32[8,128]{1,0:T(8,128)S(1)} custom-call(bf16[16,128,512]{2,1,0:T(8,128)(2,1)S(1)} %get-tuple-element.24.grad, bf16[1,16,128,512]{3,2,1,0:T(8,128)(2,1)S(1)} %copy-done, bf16[3,512,512]{2,1,0:T(8,128)(2,1)S(1)} %copy-done.1), custom_call_target="tpu_custom_call" | custom-call | flops 3221225472 | bytes 6291456 | tf_op jit(solution)/shard_map/gain_gradient/pallas_call | solution.py:367
  39.2 0.0 collective-permute-done.received
  39.2 0.2 pair_sum.1
  39.3 27.3 %all_to_all.15.received = f32[32,104,128]{2,1,0:T(8,128)S(1)} all-to-all(f32[32,104,128]{2,1,0:T(8,128)S(1)} %get-tuple-element.25), channel_id=1, replica_groups=mesh['x'=4,'yh'=2,'zh'=4,'zl'=2,'yl'=2,'core'=2] {'x','yh','zl','yl'}, dimensions={0} | all-to-all | bytes 3407872 | tf_op jit(solution)/shard_map/all_to_all | solution.py:478
  66.7 0.1 peer_sum.1.own
  66.8 5.2 %collective-permute-start.3 = (f32[112,128]{1,0:T(8,128)S(1)}, f32[112,128]{1,0:T(8,128)S(1)}, u32[]{:S(2)}, u32[]{:S(2)}) collective-permute-start(f32[112,128]{1,0:T(8,128)S(1)} %peer_sum.1.own), channel_id=1, source_target_pairs={{0,24},{8,0},{16,8},{24,16},{1,25},{9,1},{17,9},{25,17},{2,26},{10... | collective-permute-start | bytes 172040 | tf_op jit(solution)/shard_map/ppermute | solution.py:480
  72.0 1.2 collective-permute-start.2
  73.1 2.1 %collective-permute-start.1 = (f32[112,128]{1,0:T(8,128)S(1)}, f32[112,128]{1,0:T(8,128)S(1)}, u32[]{:S(2)}, u32[]{:S(2)}) collective-permute-start(f32[112,128]{1,0:T(8,128)S(1)} %peer_sum.1.own), channel_id=1, source_target_pairs={{0,8},{8,16},{16,24},{24,0},{1,9},{9,17},{17,25},{25,1},{2,10},{10... | collective-permute-start | bytes 172040 | tf_op jit(solution)/shard_map/ppermute | solution.py:480
  75.2 0.0 collective-permute-done.3.before
  75.2 3.7 %collective-permute-done.2.across = f32[112,128]{1,0:T(8,128)S(1)} collective-permute-done((f32[112,128]{1,0:T(8,128)S(1)}, f32[112,128]{1,0:T(8,128)S(1)}, u32[]{:S(2)}, u32[]{:S(2)}) %collective-permute-start.2) | collective-permute-done | bytes 57376 | tf_op jit(solution)/shard_map/ppermute | solution.py:480
  78.9 0.0 collective-permute-done.1.after
  78.9 0.1 stack_sum.1
  79.0 27.7 %all_to_all.16.rows = f32[32,112,128]{2,1,0:T(8,128)S(1)} all-to-all(f32[32,112,128]{2,1,0:T(8,128)S(1)} %stack_sum.1), channel_id=1, replica_groups=mesh['x'=4,'yh'=2,'zh'=4,'zl'=2,'yl'=2,'core'=2] {'x','yh','zl','yl'}, dimensions={0} | all-to-all | bytes 3670016 | tf_op jit(solution)/shard_map/all_to_all | solution.py:484
  106.7 4.9 %collective-permute-start.4 = (f32[32,112,128]{2,1,0:T(8,128)S(1)}, f32[32,112,128]{2,1,0:T(8,128)S(1)}, u32[]{:S(2)}, u32[]{:S(2)}) collective-permute-start(f32[32,112,128]{2,1,0:T(8,128)S(1)} %all_to_all.16.rows), channel_id=1, source_target_pairs={{0,1},{1,0},{2,3},{3,2},{4,5},{5,4},{6,7},{7,6},{8,9},{9,8},{10,11... | collective-permute-start | bytes 5505032 | tf_op jit(solution)/shard_map/ppermute | solution.py:485
  111.7 1.8 %place_mine.1 = (f32[3,32,16,512]{3,2,1,0:T(8,128)}, f32[2,32,8,128]{3,2,1,0:T(8,128)}, f32[8,128]{1,0:T(8,128)S(1)}) custom-call(s32[2]{0:T(128)S(1)} %pad_add_fusion.places, f32[32,112,128]{2,1,0:T(8,128)S(1)} %all_to_all.16.rows), custom_call_target="tpu_custom_call" | custom-call | flops 1048576 | bytes 4194304 | tf_op jit(solution)/shard_map/place_mine/pallas_call | solution.py:443
  113.5 1.6 %collective-permute-done.4.rows = f32[32,112,128]{2,1,0:T(8,128)S(1)} collective-permute-done((f32[32,112,128]{2,1,0:T(8,128)S(1)}, f32[32,112,128]{2,1,0:T(8,128)S(1)}, u32[]{:S(2)}, u32[]{:S(2)}) %collective-permute-start.4) | collective-permute-done | bytes 1835040 | tf_op jit(solution)/shard_map/ppermute | solution.py:485
  115.1 2.4 %place_other.1 = (f32[3,32,16,512]{3,2,1,0:T(8,128)}, f32[2,32,8,128]{3,2,1,0:T(8,128)}, f32[4,128]{1,0:T(4,128)}) custom-call(s32[2]{0:T(128)S(1)} %pad_add_fusion.places, f32[32,112,128]{2,1,0:T(8,128)S(1)} %collective-permute-done.4.rows, f32[8,128]{1,0:T(8,128)S(1)} %get-tuple-element.27.refs_0_, ...), custom_call_target="tpu_custom_call", output_to_operand_aliasing={{0}: (3, {}), {1}: (4, {})} | custom-call | flops 1048576 | bytes 4194304 | tf_op jit(solution)/shard_map/place_other/pallas_call | solution.py:443
Async XLA Ops:
  10.6 14.1 %all-to-all-start = ((f32[8,24,128]{2,1,0:T(8,128)}), f32[8,24,128]{2,1,0:T(8,128)S(1)}, u32[]{:S(2)}, u32[]{:S(2)}) async-start(f32[8,24,128]{2,1,0:T(8,128)} %get-tuple-element.18), calls=%async_computation | async-start | bytes 196608 | tf_op jit(solution)/shard_map/all_to_all | solution.py:466
  24.7 1.0 copy-start.2
  25.7 9.7 %copy-start = (bf16[1,16,128,512]{3,2,1,0:T(8,128)(2,1)S(1)}, bf16[1,16,128,512]{3,2,1,0:T(8,128)(2,1)}, u32[]{:S(2)}) copy-start(bf16[1,16,128,512]{3,2,1,0:T(8,128)(2,1)} %segments.1) | copy-start | bytes 6291460
  25.7 9.7 %copy-start.1 = (bf16[3,512,512]{2,1,0:T(8,128)(2,1)S(1)}, bf16[3,512,512]{2,1,0:T(8,128)(2,1)}, u32[]{:S(2)}) copy-start(bf16[3,512,512]{2,1,0:T(8,128)(2,1)} %weight.1) | copy-start | bytes 4718596
  33.2 6.0 %collective-permute-start = (f32[32,104,128]{2,1,0:T(8,128)S(1)}, f32[32,104,128]{2,1,0:T(8,128)S(1)}, u32[]{:S(2)}, u32[]{:S(2)}) collective-permute-start(f32[32,104,128]{2,1,0:T(8,128)S(1)} %get-tuple-element.23), channel_id=1, source_target_pairs={{0,1},{1,0},{2,3},{3,2},{4,5},{5,4},{6,7},{7,6},{8,9},{9,8},{10,11... | collective-permute-start | bytes 5111816 | tf_op jit(solution)/shard_map/ppermute | solution.py:468
  66.8 8.4 %collective-permute-start.3 = (f32[112,128]{1,0:T(8,128)S(1)}, f32[112,128]{1,0:T(8,128)S(1)}, u32[]{:S(2)}, u32[]{:S(2)}) collective-permute-start(f32[112,128]{1,0:T(8,128)S(1)} %peer_sum.1.own), channel_id=1, source_target_pairs={{0,24},{8,0},{16,8},{24,16},{1,25},{9,1},{17,9},{25,17},{2,26},{10... | collective-permute-start | bytes 172040 | tf_op jit(solution)/shard_map/ppermute | solution.py:480
  72.0 6.9 %collective-permute-start.2 = (f32[112,128]{1,0:T(8,128)S(1)}, f32[112,128]{1,0:T(8,128)S(1)}, u32[]{:S(2)}, u32[]{:S(2)}) collective-permute-start(f32[112,128]{1,0:T(8,128)S(1)} %peer_sum.1.own), channel_id=1, source_target_pairs={{0,16},{8,24},{16,0},{24,8},{1,17},{9,25},{17,1},{25,9},{2,18},{10... | collective-permute-start | bytes 172040 | tf_op jit(solution)/shard_map/ppermute | solution.py:480
  73.1 5.8 %collective-permute-start.1 = (f32[112,128]{1,0:T(8,128)S(1)}, f32[112,128]{1,0:T(8,128)S(1)}, u32[]{:S(2)}, u32[]{:S(2)}) collective-permute-start(f32[112,128]{1,0:T(8,128)S(1)} %peer_sum.1.own), channel_id=1, source_target_pairs={{0,8},{8,16},{16,24},{24,0},{1,9},{9,17},{17,25},{25,1},{2,10},{10... | collective-permute-start | bytes 172040 | tf_op jit(solution)/shard_map/ppermute | solution.py:480
  106.7 8.4 %collective-permute-start.4 = (f32[32,112,128]{2,1,0:T(8,128)S(1)}, f32[32,112,128]{2,1,0:T(8,128)S(1)}, u32[]{:S(2)}, u32[]{:S(2)}) collective-permute-start(f32[32,112,128]{2,1,0:T(8,128)S(1)} %all_to_all.16.rows), channel_id=1, source_target_pairs={{0,1},{1,0},{2,3},{3,2},{4,5},{5,4},{6,7},{7,6},{8,9},{9,8},{10,11... | collective-permute-start | bytes 5505032 | tf_op jit(solution)/shard_map/ppermute | solution.py:485

commit v5 on v4

--- a/solution.py
+++ b/solution.py
@@ -69,8 +69,9 @@
 
 def forward_kernel(
     group_hbm, positive_hbm, segments_hbm, weight_hbm, gain_hbm, head_hbm,
-    normed_hbm, slope_hbm, pack_out, send_out,
-    group, positive, segments, weight, gain, head, pooled, normed_out, slope_out, step_sems, out_sems, sems,
+    normed_hbm, slope_hbm, pack_hbm, send_hbm,
+    group, positive, segments, weight, gain, head, pooled, normed_out, slope_out, pack_out, send_out,
+    step_sems, out_sems, sems,
 ):
     cubic = 0.044715
     scale = 0.7978845608028654
@@ -91,6 +92,10 @@
     head_copy = pltpu.make_async_copy(head_hbm, head, sems.at[2])
     group_copy = pltpu.make_async_copy(group_hbm, group, sems.at[3])
     positive_copy = pltpu.make_async_copy(positive_hbm, positive, sems.at[4])
+    start_rows, head_rows = pl.ds(0, PACK_HEAD), pl.ds(PACK_HEAD, C)
+    head_store = pltpu.make_async_copy(pack_out.at[head_rows], pack_hbm.at[head_rows], sems.at[5])
+    pack_store = pltpu.make_async_copy(pack_out.at[start_rows], pack_hbm.at[start_rows], sems.at[6])
+    send_store = pltpu.make_async_copy(send_out, send_hbm, sems.at[7])
     gain_copy.start()
     fetch(0).start()
     weight_copy.start()
@@ -134,6 +139,8 @@
 
     lax.fori_loop(0, F_STEPS, one_step, 0)
     head_copy.wait()
+    pack_out[PACK_HEAD:, :] = head[...].astype(jnp.float32)
+    head_store.start()
     group_copy.wait()
     positive_copy.wait()
     rounded = pooled[...].astype(jnp.bfloat16)
@@ -145,7 +152,6 @@
     for block in range(C // 128):
         at = PACK_POOLED + block * SEGS
         pack_out[at : at + SEGS, :] = rounded[:, block * 128 : (block + 1) * 128].astype(jnp.float32)
-    pack_out[PACK_HEAD:, :] = head[...].astype(jnp.float32)
     embedding = unit_rows(projected) * PROJ ** (-0.5)
     lane = lax.broadcasted_iota(jnp.int32, (8, 128), 1) & (SEGS - 1)
     groups = jnp.zeros((8, 128), jnp.int32)
@@ -155,6 +161,11 @@
     for rank in range(RANKS):
         send_out[rank, 0:SEGS, :] = embedding
         send_out[rank, SEGS:, :] = groups
+    send_store.start()
+    pack_store.start()
+    head_store.wait()
+    send_store.wait()
+    pack_store.wait()
     for step in range(F_STEPS):
         for copy in store(step):
             copy.wait()
@@ -166,7 +177,7 @@
     return pl.pallas_call(
         forward_kernel,
         in_specs=[IN_HBM] * 6,
-        out_specs=[IN_HBM] * 2 + [IN_VMEM] * 2,
+        out_specs=[IN_HBM] * 4,
         out_shape=[
             jax.ShapeDtypeStruct((SEGS, LEN, C), bf16),
             jax.ShapeDtypeStruct((SEGS, LEN, C), f32),
@@ -183,9 +194,11 @@
             VMEM((SEGS, C), f32),
             VMEM((SEGS, LEN, C), bf16),
             VMEM((SEGS, LEN, C), f32),
+            VMEM((PACK, PROJ), f32),
+            VMEM((RANKS, SEGS + 8, PROJ), f32),
             DMA((F_STEPS,)),
             DMA((2, F_STEPS)),
-            DMA((5,)),
+            DMA((8,)),
         ],
         compiler_params=pltpu.CompilerParams(vmem_limit_bytes=FULL),
         cost_estimate=pl.CostEstimate(flops=2 * SEGS * LEN * TAPS * C * C, bytes_accessed=10 << 20, transcendentals=SEGS * LEN * C),
@@ -413,7 +426,7 @@
 
 def place_kernel(flip, places, rows, *refs):
     gain_before = refs[0] if flip else None
-    conv_hbm, head_hbm, gain_out, sems = refs[-4:]
+    conv_hbm, head_hbm, gain_out, sems = refs[3:7] if flip else refs
     wide = C // 128
     half = 1 - places[1] if flip else places[1]
     copies = []
@@ -431,7 +444,10 @@
     for peer in range(1, PEERS):
         summed = summed + rows[peer, CHUNK:, :]
     if flip:
-        gain_out[...] = (summed + gain_before[...])[0:wide, :]
+        gain_sum = refs[7]
+        gain_sum[...] = (summed + gain_before[...])[0:wide, :]
+        copies.append(pltpu.make_async_copy(gain_sum, gain_out, sems.at[HALF + 1]))
+        copies[-1].start()
     else:
         gain_out[...] = summed
     for copy in copies:
@@ -443,13 +459,13 @@
     return pl.pallas_call(
         functools.partial(place_kernel, flip),
         in_specs=[IN_SMEM, IN_VMEM] + ([IN_VMEM, IN_HBM, IN_HBM] if flip else []),
-        out_specs=[IN_HBM, IN_HBM, IN_VMEM],
+        out_specs=[IN_HBM, IN_HBM, IN_HBM if flip else IN_VMEM],
         out_shape=(
             jax.ShapeDtypeStruct((TAPS, PEERS, EACH, C), f32),
             jax.ShapeDtypeStruct((2, PEERS, PROJ_ROWS, PROJ), f32),
             jax.ShapeDtypeStruct((C // 128 if flip else GAIN_ROWS, 128), f32),
         ),
-        scratch_shapes=[DMA((HALF + 1,))],
+        scratch_shapes=[DMA((HALF + 2,))] + ([VMEM((C // 128, 128), f32)] if flip else []),
         input_output_aliases={3: 0, 4: 1} if flip else {},
         compiler_params=pltpu.CompilerParams(vmem_limit_bytes=24 << 20),
         cost_estimate=pl.CostEstimate(flops=1 << 20, bytes_accessed=4 << 20, transcendentals=0),
@@ -464,6 +480,7 @@
     places = jnp.stack([lax.axis_index(("x", "yh")), lax.axis_index("core")]).astype(jnp.int32)
     normed, slope, pack, send = forward(group, positive, segments, conv_weight, gain.reshape(1, C), head)
     gathered = lax.all_to_all(send, ("x", "yh"), 0, 0)
+    pack = jnp.where(places[1] >= 0, pack, 0.0)
     grad, keep, give = weight_gradient(places, gathered, pack, normed, slope)
     received = lax.ppermute(give, "core", swap)
     gain_part = gain_gradient(grad, segments, conv_weight)

time: 118 us -> 116 us (0.983)
  transfers between devices with their start and end apart: 6 -> 6, of which waited for: 3 -> 3; matrix products, arithmetic and copies ran while one was open for 0% -> 1% of each run, Pallas kernels for 5% -> 5%
where the time goes in v5:
time: 116 us; the launch traced here: 115 us
  blocking collectives  55 us (47%)
  Pallas kernels  24.6 us (21%)
  starting transfers between devices  23.1 us (20%)
  waiting for transfers between devices  10.9 us (9%)
    all_to_all x1, blocking collectives, body(): mine = lax.all_to_all(spread, peers, 0, 0)  27.7 us
    all_to_all x1, blocking collectives, body(): across = lax.all_to_all(paired, peers, 0, 0)  27.3 us
    pallas_call x1, Pallas kernels, forward(): pl.pallas_call(forward_kernel, in_specs=[IN_HBM] * 6, out_specs=[IN_HBM]...  9.31 us
    ppermute x3, starting transfers between devices, body(): lax.ppermute(chunk, 'zh', [(i, (i + d) % STACKS) for i in range(STACKS)])  8.44 us
    all_to_all x1, starting transfers between devices, body(): gathered = lax.all_to_all(send, ('x', 'yh'), 0, 0)  7.48 us
    pallas_call x1, Pallas kernels, weight_gradient(): pl.pallas_call(weight_kernel, in_specs=[IN_SMEM, IN_VMEM, IN_VMEM, IN_HBM...  7.48 us
    all_to_all x1, waiting for transfers between devices, body(): gathered = lax.all_to_all(send, ('x', 'yh'), 0, 0)  5.59 us
    ppermute x1, starting transfers between devices, body(): other = lax.ppermute(mine, 'core', swap)  4.95 us
  transfers between devices with their start and end apart: 6, of which 3 were waited for; matrix products, arithmetic and copies ran while one was open for 1% of the time, Pallas kernels for 5%

profile of v5, /device:TPU:1, one launch (start us, length us, event | category | flops | bytes accessed | tf_op | source)
XLA Modules:
  0.0 115.4 jit_solution(1716821342587905139)
XLA Ops:
  0.6 9.3 %forward.1 = (bf16[16,128,512]{2,1,0:T(8,128)(2,1)}, f32[16,128,512]{2,1,0:T(8,128)}, f32[608,128]{1,0:T(8,128)}, f32[8,24,128]{2,1,0:T(8,128)}) custom-call(s32[1,16]{1,0:T(1,128)} %group_hbm.1, s32[1,16]{1,0:T(1,128)} %positive_hbm.1, bf16[1,16,128,512]{3,2,1,0:T(8,128)(2,1)} %segments.1, bf16[1536,512]{1,0:T(8,128)(2,1)} %bitcast.7, f32[1,512]{1,0:T(1,128)} %bitcast.10, ...), custom_call_target="tpu_custom_call" | custom-call | flops 3221225472 | bytes 10485760 | tf_op jit(solution)/shard_map/forward/pallas_call | solution.py:177
  10.0 7.5 %all-to-all-start = ((f32[8,24,128]{2,1,0:T(8,128)}), f32[8,24,128]{2,1,0:T(8,128)S(1)}, u32[]{:S(2)}, u32[]{:S(2)}) async-start(f32[8,24,128]{2,1,0:T(8,128)} %get-tuple-element.18), calls=%async_computation | async-start | bytes 196608 | tf_op jit(solution)/shard_map/all_to_all | solution.py:482
  17.4 1.0 broadcast_select_fusion.pack
  18.4 0.1 pad_add_fusion.places
  18.5 5.6 %all-to-all-done.gathered = f32[8,24,128]{2,1,0:T(8,128)S(1)} async-done(((f32[8,24,128]{2,1,0:T(8,128)}), f32[8,24,128]{2,1,0:T(8,128)S(1)}, u32[]{:S(2)}, u32[]{:S(2)}) %all-to-all-start) | async-done | bytes 98336 | tf_op jit(solution)/shard_map/all_to_all | solution.py:482
  24.1 0.0 copy-start
  24.1 0.0 copy-start.1
  24.1 7.5 %weight_gradient.1 = (bf16[16,128,512]{2,1,0:T(8,128)(2,1)S(1)}, f32[32,104,128]{2,1,0:T(8,128)S(1)}, f32[32,104,128]{2,1,0:T(8,128)S(1)}) custom-call(s32[2]{0:T(128)S(1)} %pad_add_fusion.places, f32[8,24,128]{2,1,0:T(8,128)S(1)} %all-to-all-done.gathered, f32[608,128]{1,0:T(8,128)S(1)} %broadcast_select_fusion.pack, ...), custom_call_target="tpu_custom_call" | custom-call | flops 3221225472 | bytes 12582912 | tf_op jit(solution)/shard_map/weight_gradient/pallas_call | solution.py:323
  31.6 2.2 %collective-permute-start = (f32[32,104,128]{2,1,0:T(8,128)S(1)}, f32[32,104,128]{2,1,0:T(8,128)S(1)}, u32[]{:S(2)}, u32[]{:S(2)}) collective-permute-start(f32[32,104,128]{2,1,0:T(8,128)S(1)} %get-tuple-element.23), channel_id=1, source_target_pairs={{0,1},{1,0},{2,3},{3,2},{4,5},{5,4},{6,7},{7,6},{8,9},{9,8},{10,11... | collective-permute-start | bytes 5111816 | tf_op jit(solution)/shard_map/ppermute | solution.py:485
  33.8 0.0 copy-done
  33.8 0.0 copy-done.1
  33.8 3.9 %gain_gradient.1.gain = f32[8,128]{1,0:T(8,128)S(1)} custom-call(bf16[16,128,512]{2,1,0:T(8,128)(2,1)S(1)} %get-tuple-element.24.grad, bf16[1,16,128,512]{3,2,1,0:T(8,128)(2,1)S(1)} %copy-done, bf16[3,512,512]{2,1,0:T(8,128)(2,1)S(1)} %copy-done.1), custom_call_target="tpu_custom_call" | custom-call | flops 3221225472 | bytes 6291456 | tf_op jit(solution)/shard_map/gain_gradient/pallas_call | solution.py:380
  37.6 0.0 collective-permute-done.received
  37.7 0.2 pair_sum.1
  37.8 27.3 %all_to_all.15.received = f32[32,104,128]{2,1,0:T(8,128)S(1)} all-to-all(f32[32,104,128]{2,1,0:T(8,128)S(1)} %get-tuple-element.25), channel_id=1, replica_groups=mesh['x'=4,'yh'=2,'zh'=4,'zl'=2,'yl'=2,'core'=2] {'x','yh','zl','yl'}, dimensions={0} | all-to-all | bytes 3407872 | tf_op jit(solution)/shard_map/all_to_all | solution.py:495
  65.2 0.1 peer_sum.1.own
  65.3 5.2 %collective-permute-start.3 = (f32[112,128]{1,0:T(8,128)S(1)}, f32[112,128]{1,0:T(8,128)S(1)}, u32[]{:S(2)}, u32[]{:S(2)}) collective-permute-start(f32[112,128]{1,0:T(8,128)S(1)} %peer_sum.1.own), channel_id=1, source_target_pairs={{0,24},{8,0},{16,8},{24,16},{1,25},{9,1},{17,9},{25,17},{2,26},{10... | collective-permute-start | bytes 172040 | tf_op jit(solution)/shard_map/ppermute | solution.py:497
  70.5 1.2 %collective-permute-start.2 = (f32[112,128]{1,0:T(8,128)S(1)}, f32[112,128]{1,0:T(8,128)S(1)}, u32[]{:S(2)}, u32[]{:S(2)}) collective-permute-start(f32[112,128]{1,0:T(8,128)S(1)} %peer_sum.1.own), channel_id=1, source_target_pairs={{0,16},{8,24},{16,0},{24,8},{1,17},{9,25},{17,1},{25,9},{2,18},{10... | collective-permute-start | bytes 172040 | tf_op jit(solution)/shard_map/ppermute | solution.py:497
  71.6 2.1 %collective-permute-start.1 = (f32[112,128]{1,0:T(8,128)S(1)}, f32[112,128]{1,0:T(8,128)S(1)}, u32[]{:S(2)}, u32[]{:S(2)}) collective-permute-start(f32[112,128]{1,0:T(8,128)S(1)} %peer_sum.1.own), channel_id=1, source_target_pairs={{0,8},{8,16},{16,24},{24,0},{1,9},{9,17},{17,25},{25,1},{2,10},{10... | collective-permute-start | bytes 172040 | tf_op jit(solution)/shard_map/ppermute | solution.py:497
  73.7 0.0 collective-permute-done.3.before
  73.7 3.7 %collective-permute-done.2.across = f32[112,128]{1,0:T(8,128)S(1)} collective-permute-done((f32[112,128]{1,0:T(8,128)S(1)}, f32[112,128]{1,0:T(8,128)S(1)}, u32[]{:S(2)}, u32[]{:S(2)}) %collective-permute-start.2) | collective-permute-done | bytes 57376 | tf_op jit(solution)/shard_map/ppermute | solution.py:497
  77.4 0.0 collective-permute-done.1.after
  77.4 0.1 stack_sum.1
  77.5 27.7 %all_to_all.16.rows = f32[32,112,128]{2,1,0:T(8,128)S(1)} all-to-all(f32[32,112,128]{2,1,0:T(8,128)S(1)} %stack_sum.1), channel_id=1, replica_groups=mesh['x'=4,'yh'=2,'zh'=4,'zl'=2,'yl'=2,'core'=2] {'x','yh','zl','yl'}, dimensions={0} | all-to-all | bytes 3670016 | tf_op jit(solution)/shard_map/all_to_all | solution.py:501
  105.2 4.9 %collective-permute-start.4 = (f32[32,112,128]{2,1,0:T(8,128)S(1)}, f32[32,112,128]{2,1,0:T(8,128)S(1)}, u32[]{:S(2)}, u32[]{:S(2)}) collective-permute-start(f32[32,112,128]{2,1,0:T(8,128)S(1)} %all_to_all.16.rows), channel_id=1, source_target_pairs={{0,1},{1,0},{2,3},{3,2},{4,5},{5,4},{6,7},{7,6},{8,9},{9,8},{10,11... | collective-permute-start | bytes 5505032 | tf_op jit(solution)/shard_map/ppermute | solution.py:502
  110.2 1.8 %place_mine.1 = (f32[3,32,16,512]{3,2,1,0:T(8,128)}, f32[2,32,8,128]{3,2,1,0:T(8,128)}, f32[8,128]{1,0:T(8,128)S(1)}) custom-call(s32[2]{0:T(128)S(1)} %pad_add_fusion.places, f32[32,112,128]{2,1,0:T(8,128)S(1)} %all_to_all.16.rows), custom_call_target="tpu_custom_call" | custom-call | flops 1048576 | bytes 4194304 | tf_op jit(solution)/shard_map/place_mine/pallas_call | solution.py:459
  112.0 1.6 %collective-permute-done.4.rows = f32[32,112,128]{2,1,0:T(8,128)S(1)} collective-permute-done((f32[32,112,128]{2,1,0:T(8,128)S(1)}, f32[32,112,128]{2,1,0:T(8,128)S(1)}, u32[]{:S(2)}, u32[]{:S(2)}) %collective-permute-start.4) | collective-permute-done | bytes 1835040 | tf_op jit(solution)/shard_map/ppermute | solution.py:502
  113.6 1.8 %place_other.1 = (f32[3,32,16,512]{3,2,1,0:T(8,128)}, f32[2,32,8,128]{3,2,1,0:T(8,128)}, f32[4,128]{1,0:T(4,128)}) custom-call(s32[2]{0:T(128)S(1)} %pad_add_fusion.places, f32[32,112,128]{2,1,0:T(8,128)S(1)} %collective-permute-done.4.rows, f32[8,128]{1,0:T(8,128)S(1)} %get-tuple-element.27.refs_0_, ...), custom_call_target="tpu_custom_call", output_to_operand_aliasing={{0}: (3, {}), {1}: (4, {})} | custom-call | flops 1048576 | bytes 4194304 | tf_op jit(solution)/shard_map/place_other/pallas_call | solution.py:459
Async XLA Ops:
  10.0 14.1 %all-to-all-start = ((f32[8,24,128]{2,1,0:T(8,128)}), f32[8,24,128]{2,1,0:T(8,128)S(1)}, u32[]{:S(2)}, u32[]{:S(2)}) async-start(f32[8,24,128]{2,1,0:T(8,128)} %get-tuple-element.18), calls=%async_computation | async-start | bytes 196608 | tf_op jit(solution)/shard_map/all_to_all | solution.py:482
  24.1 9.7 %copy-start = (bf16[1,16,128,512]{3,2,1,0:T(8,128)(2,1)S(1)}, bf16[1,16,128,512]{3,2,1,0:T(8,128)(2,1)}, u32[]{:S(2)}) copy-start(bf16[1,16,128,512]{3,2,1,0:T(8,128)(2,1)} %segments.1) | copy-start | bytes 6291460
  24.1 9.7 %copy-start.1 = (bf16[3,512,512]{2,1,0:T(8,128)(2,1)S(1)}, bf16[3,512,512]{2,1,0:T(8,128)(2,1)}, u32[]{:S(2)}) copy-start(bf16[3,512,512]{2,1,0:T(8,128)(2,1)} %weight.1) | copy-start | bytes 4718596
  31.6 6.1 %collective-permute-start = (f32[32,104,128]{2,1,0:T(8,128)S(1)}, f32[32,104,128]{2,1,0:T(8,128)S(1)}, u32[]{:S(2)}, u32[]{:S(2)}) collective-permute-start(f32[32,104,128]{2,1,0:T(8,128)S(1)} %get-tuple-element.23), channel_id=1, source_target_pairs={{0,1},{1,0},{2,3},{3,2},{4,5},{5,4},{6,7},{7,6},{8,9},{9,8},{10,11... | collective-permute-start | bytes 5111816 | tf_op jit(solution)/shard_map/ppermute | solution.py:485
  65.3 8.4 %collective-permute-start.3 = (f32[112,128]{1,0:T(8,128)S(1)}, f32[112,128]{1,0:T(8,128)S(1)}, u32[]{:S(2)}, u32[]{:S(2)}) collective-permute-start(f32[112,128]{1,0:T(8,128)S(1)} %peer_sum.1.own), channel_id=1, source_target_pairs={{0,24},{8,0},{16,8},{24,16},{1,25},{9,1},{17,9},{25,17},{2,26},{10... | collective-permute-start | bytes 172040 | tf_op jit(solution)/shard_map/ppermute | solution.py:497
  70.5 6.9 %collective-permute-start.2 = (f32[112,128]{1,0:T(8,128)S(1)}, f32[112,128]{1,0:T(8,128)S(1)}, u32[]{:S(2)}, u32[]{:S(2)}) collective-permute-start(f32[112,128]{1,0:T(8,128)S(1)} %peer_sum.1.own), channel_id=1, source_target_pairs={{0,16},{8,24},{16,0},{24,8},{1,17},{9,25},{17,1},{25,9},{2,18},{10... | collective-permute-start | bytes 172040 | tf_op jit(solution)/shard_map/ppermute | solution.py:497
  71.6 5.8 %collective-permute-start.1 = (f32[112,128]{1,0:T(8,128)S(1)}, f32[112,128]{1,0:T(8,128)S(1)}, u32[]{:S(2)}, u32[]{:S(2)}) collective-permute-start(f32[112,128]{1,0:T(8,128)S(1)} %peer_sum.1.own), channel_id=1, source_target_pairs={{0,8},{8,16},{16,24},{24,0},{1,9},{9,17},{17,25},{25,1},{2,10},{10... | collective-permute-start | bytes 172040 | tf_op jit(solution)/shard_map/ppermute | solution.py:497
  105.2 8.4 %collective-permute-start.4 = (f32[32,112,128]{2,1,0:T(8,128)S(1)}, f32[32,112,128]{2,1,0:T(8,128)S(1)}, u32[]{:S(2)}, u32[]{:S(2)}) collective-permute-start(f32[32,112,128]{2,1,0:T(8,128)S(1)} %all_to_all.16.rows), channel_id=1, source_target_pairs={{0,1},{1,0},{2,3},{3,2},{4,5},{5,4},{6,7},{7,6},{8,9},{9,8},{10,11... | collective-permute-start | bytes 5505032 | tf_op jit(solution)/shard_map/ppermute | solution.py:502

commit v6 on v5

--- a/solution.py
+++ b/solution.py
@@ -475,7 +475,7 @@
 
 def body(segments, conv_weight, gain, head, group, positive):
     f32 = jnp.float32
-    peers = ("x", "yh", "zl", "yl")
+    peers = ("zl", "yh", "yl", "x")
     swap = [(0, 1), (1, 0)]
     places = jnp.stack([lax.axis_index(("x", "yh")), lax.axis_index("core")]).astype(jnp.int32)
     normed, slope, pack, send = forward(group, positive, segments, conv_weight, gain.reshape(1, C), head)

time: 116 us -> 115 us (level)
  transfers between devices with their start and end apart: 6 -> 6, of which waited for: 3 -> 4; matrix products, arithmetic and copies ran while one was open for 1% -> 1% of each run, Pallas kernels for 5% -> 5%
where the time goes in v6:
time: 115 us
  blocking collectives  54.9 us (48%)
  Pallas kernels  24.6 us (21%)
  starting transfers between devices  22.2 us (19%)
  waiting for transfers between devices  11.5 us (10%)
    all_to_all x1, blocking collectives, body(): mine = lax.all_to_all(spread, peers, 0, 0)  27.7 us
    all_to_all x1, blocking collectives, body(): across = lax.all_to_all(paired, peers, 0, 0)  27.2 us
    pallas_call x1, Pallas kernels, forward(): pl.pallas_call(forward_kernel, in_specs=[IN_HBM] * 6, out_specs=[IN_HBM]...  9.31 us
    ppermute x3, starting transfers between devices, body(): lax.ppermute(chunk, 'zh', [(i, (i + d) % STACKS) for i in range(STACKS)])  8.44 us
    all_to_all x1, starting transfers between devices, body(): gathered = lax.all_to_all(send, ('x', 'yh'), 0, 0)  7.48 us
    pallas_call x1, Pallas kernels, weight_gradient(): pl.pallas_call(weight_kernel, in_specs=[IN_SMEM, IN_VMEM, IN_VMEM, IN_HBM...  7.48 us
    all_to_all x1, waiting for transfers between devices, body(): gathered = lax.all_to_all(send, ('x', 'yh'), 0, 0)  5.59 us
    ppermute x3, waiting for transfers between devices, body(): lax.ppermute(chunk, 'zh', [(i, (i + d) % STACKS) for i in range(STACKS)])  4.29 us
  transfers between devices with their start and end apart: 6, of which 4 were waited for; matrix products, arithmetic and copies ran while one was open for 1% of the time, Pallas kernels for 5%

profile of v6, /device:TPU:1, one launch (start us, length us, event | category | flops | bytes accessed | tf_op | source)
XLA Modules:
  0.0 115.0 jit_solution(16781504582845684751)
XLA Ops:
  0.6 9.3 %forward.1 = (bf16[16,128,512]{2,1,0:T(8,128)(2,1)}, f32[16,128,512]{2,1,0:T(8,128)}, f32[608,128]{1,0:T(8,128)}, f32[8,24,128]{2,1,0:T(8,128)}) custom-call(s32[1,16]{1,0:T(1,128)} %group_hbm.1, s32[1,16]{1,0:T(1,128)} %positive_hbm.1, bf16[1,16,128,512]{3,2,1,0:T(8,128)(2,1)} %segments.1, bf16[1536,512]{1,0:T(8,128)(2,1)} %bitcast.7, f32[1,512]{1,0:T(1,128)} %bitcast.10, ...), custom_call_target="tpu_custom_call" | custom-call | flops 3221225472 | bytes 10485760 | tf_op jit(solution)/shard_map/forward/pallas_call | solution.py:177
  10.0 7.5 %all-to-all-start = ((f32[8,24,128]{2,1,0:T(8,128)}), f32[8,24,128]{2,1,0:T(8,128)S(1)}, u32[]{:S(2)}, u32[]{:S(2)}) async-start(f32[8,24,128]{2,1,0:T(8,128)} %get-tuple-element.18), calls=%async_computation | async-start | bytes 196608 | tf_op jit(solution)/shard_map/all_to_all | solution.py:482
  17.4 1.0 broadcast_select_fusion.pack
  18.4 0.1 pad_add_fusion.places
  18.5 5.6 %all-to-all-done.gathered = f32[8,24,128]{2,1,0:T(8,128)S(1)} async-done(((f32[8,24,128]{2,1,0:T(8,128)}), f32[8,24,128]{2,1,0:T(8,128)S(1)}, u32[]{:S(2)}, u32[]{:S(2)}) %all-to-all-start) | async-done | bytes 98336 | tf_op jit(solution)/shard_map/all_to_all | solution.py:482
  24.1 0.0 copy-start
  24.1 0.0 copy-start.1
  24.1 7.5 %weight_gradient.1 = (bf16[16,128,512]{2,1,0:T(8,128)(2,1)S(1)}, f32[32,104,128]{2,1,0:T(8,128)S(1)}, f32[32,104,128]{2,1,0:T(8,128)S(1)}) custom-call(s32[2]{0:T(128)S(1)} %pad_add_fusion.places, f32[8,24,128]{2,1,0:T(8,128)S(1)} %all-to-all-done.gathered, f32[608,128]{1,0:T(8,128)S(1)} %broadcast_select_fusion.pack, ...), custom_call_target="tpu_custom_call" | custom-call | flops 3221225472 | bytes 12582912 | tf_op jit(solution)/shard_map/weight_gradient/pallas_call | solution.py:323
  31.6 2.2 %collective-permute-start = (f32[32,104,128]{2,1,0:T(8,128)S(1)}, f32[32,104,128]{2,1,0:T(8,128)S(1)}, u32[]{:S(2)}, u32[]{:S(2)}) collective-permute-start(f32[32,104,128]{2,1,0:T(8,128)S(1)} %get-tuple-element.23), channel_id=1, source_target_pairs={{0,1},{1,0},{2,3},{3,2},{4,5},{5,4},{6,7},{7,6},{8,9},{9,8},{10,11... | collective-permute-start | bytes 5111816 | tf_op jit(solution)/shard_map/ppermute | solution.py:485
  33.8 0.0 copy-done
  33.8 0.0 copy-done.1
  33.8 3.9 %gain_gradient.1.gain = f32[8,128]{1,0:T(8,128)S(1)} custom-call(bf16[16,128,512]{2,1,0:T(8,128)(2,1)S(1)} %get-tuple-element.24.grad, bf16[1,16,128,512]{3,2,1,0:T(8,128)(2,1)S(1)} %copy-done, bf16[3,512,512]{2,1,0:T(8,128)(2,1)S(1)} %copy-done.1), custom_call_target="tpu_custom_call" | custom-call | flops 3221225472 | bytes 6291456 | tf_op jit(solution)/shard_map/gain_gradient/pallas_call | solution.py:380
  37.6 0.0 collective-permute-done.received
  37.7 0.2 pair_sum.1
  37.8 27.2 %all_to_all.15.received = f32[32,104,128]{2,1,0:T(8,128)S(1)} all-to-all(f32[32,104,128]{2,1,0:T(8,128)S(1)} %get-tuple-element.25), channel_id=1, replica_groups=mesh['x'=4,'yh'=2,'zh'=4,'zl'=2,'yl'=2,'core'=2] {'zl','yh','yl','x'}, dimensions={0} | all-to-all | bytes 3407872 | tf_op jit(solution)/shard_map/all_to_all | solution.py:495
  65.0 0.1 peer_sum.1.own
  65.1 5.2 %collective-permute-start.3 = (f32[112,128]{1,0:T(8,128)S(1)}, f32[112,128]{1,0:T(8,128)S(1)}, u32[]{:S(2)}, u32[]{:S(2)}) collective-permute-start(f32[112,128]{1,0:T(8,128)S(1)} %peer_sum.1.own), channel_id=1, source_target_pairs={{0,24},{8,0},{16,8},{24,16},{1,25},{9,1},{17,9},{25,17},{2,26},{10... | collective-permute-start | bytes 172040 | tf_op jit(solution)/shard_map/ppermute | solution.py:497
  70.3 1.2 %collective-permute-start.2 = (f32[112,128]{1,0:T(8,128)S(1)}, f32[112,128]{1,0:T(8,128)S(1)}, u32[]{:S(2)}, u32[]{:S(2)}) collective-permute-start(f32[112,128]{1,0:T(8,128)S(1)} %peer_sum.1.own), channel_id=1, source_target_pairs={{0,16},{8,24},{16,0},{24,8},{1,17},{9,25},{17,1},{25,9},{2,18},{10... | collective-permute-start | bytes 172040 | tf_op jit(solution)/shard_map/ppermute | solution.py:497
  71.5 2.1 %collective-permute-start.1 = (f32[112,128]{1,0:T(8,128)S(1)}, f32[112,128]{1,0:T(8,128)S(1)}, u32[]{:S(2)}, u32[]{:S(2)}) collective-permute-start(f32[112,128]{1,0:T(8,128)S(1)} %peer_sum.1.own), channel_id=1, source_target_pairs={{0,8},{8,16},{16,24},{24,0},{1,9},{9,17},{17,25},{25,1},{2,10},{10... | collective-permute-start | bytes 172040 | tf_op jit(solution)/shard_map/ppermute | solution.py:497
  73.6 0.0 collective-permute-done.3.before
  73.6 3.9 %collective-permute-done.2.across = f32[112,128]{1,0:T(8,128)S(1)} collective-permute-done((f32[112,128]{1,0:T(8,128)S(1)}, f32[112,128]{1,0:T(8,128)S(1)}, u32[]{:S(2)}, u32[]{:S(2)}) %collective-permute-start.2) | collective-permute-done | bytes 57376 | tf_op jit(solution)/shard_map/ppermute | solution.py:497
  77.4 0.4 collective-permute-done.1.after
  77.8 0.1 stack_sum.1
  78.0 27.7 %all_to_all.16.rows = f32[32,112,128]{2,1,0:T(8,128)S(1)} all-to-all(f32[32,112,128]{2,1,0:T(8,128)S(1)} %stack_sum.1), channel_id=1, replica_groups=mesh['x'=4,'yh'=2,'zh'=4,'zl'=2,'yl'=2,'core'=2] {'zl','yh','yl','x'}, dimensions={0} | all-to-all | bytes 3670016 | tf_op jit(solution)/shard_map/all_to_all | solution.py:501
  105.7 4.1 %collective-permute-start.4 = (f32[32,112,128]{2,1,0:T(8,128)S(1)}, f32[32,112,128]{2,1,0:T(8,128)S(1)}, u32[]{:S(2)}, u32[]{:S(2)}) collective-permute-start(f32[32,112,128]{2,1,0:T(8,128)S(1)} %all_to_all.16.rows), channel_id=1, source_target_pairs={{0,1},{1,0},{2,3},{3,2},{4,5},{5,4},{6,7},{7,6},{8,9},{9,8},{10,11... | collective-permute-start | bytes 5505032 | tf_op jit(solution)/shard_map/ppermute | solution.py:502
  109.8 1.8 %place_mine.1 = (f32[3,32,16,512]{3,2,1,0:T(8,128)}, f32[2,32,8,128]{3,2,1,0:T(8,128)}, f32[8,128]{1,0:T(8,128)S(1)}) custom-call(s32[2]{0:T(128)S(1)} %pad_add_fusion.places, f32[32,112,128]{2,1,0:T(8,128)S(1)} %all_to_all.16.rows), custom_call_target="tpu_custom_call" | custom-call | flops 1048576 | bytes 4194304 | tf_op jit(solution)/shard_map/place_mine/pallas_call | solution.py:459
  111.6 1.6 %collective-permute-done.4.rows = f32[32,112,128]{2,1,0:T(8,128)S(1)} collective-permute-done((f32[32,112,128]{2,1,0:T(8,128)S(1)}, f32[32,112,128]{2,1,0:T(8,128)S(1)}, u32[]{:S(2)}, u32[]{:S(2)}) %collective-permute-start.4) | collective-permute-done | bytes 1835040 | tf_op jit(solution)/shard_map/ppermute | solution.py:502
  113.2 1.8 %place_other.1 = (f32[3,32,16,512]{3,2,1,0:T(8,128)}, f32[2,32,8,128]{3,2,1,0:T(8,128)}, f32[4,128]{1,0:T(4,128)}) custom-call(s32[2]{0:T(128)S(1)} %pad_add_fusion.places, f32[32,112,128]{2,1,0:T(8,128)S(1)} %collective-permute-done.4.rows, f32[8,128]{1,0:T(8,128)S(1)} %get-tuple-element.27.refs_0_, ...), custom_call_target="tpu_custom_call", output_to_operand_aliasing={{0}: (3, {}), {1}: (4, {})} | custom-call | flops 1048576 | bytes 4194304 | tf_op jit(solution)/shard_map/place_other/pallas_call | solution.py:459
Async XLA Ops:
  10.0 14.1 %all-to-all-start = ((f32[8,24,128]{2,1,0:T(8,128)}), f32[8,24,128]{2,1,0:T(8,128)S(1)}, u32[]{:S(2)}, u32[]{:S(2)}) async-start(f32[8,24,128]{2,1,0:T(8,128)} %get-tuple-element.18), calls=%async_computation | async-start | bytes 196608 | tf_op jit(solution)/shard_map/all_to_all | solution.py:482
  24.1 9.7 %copy-start = (bf16[1,16,128,512]{3,2,1,0:T(8,128)(2,1)S(1)}, bf16[1,16,128,512]{3,2,1,0:T(8,128)(2,1)}, u32[]{:S(2)}) copy-start(bf16[1,16,128,512]{3,2,1,0:T(8,128)(2,1)} %segments.1) | copy-start | bytes 6291460
  24.1 9.7 %copy-start.1 = (bf16[3,512,512]{2,1,0:T(8,128)(2,1)S(1)}, bf16[3,512,512]{2,1,0:T(8,128)(2,1)}, u32[]{:S(2)}) copy-start(bf16[3,512,512]{2,1,0:T(8,128)(2,1)} %weight.1) | copy-start | bytes 4718596
  31.6 6.1 %collective-permute-start = (f32[32,104,128]{2,1,0:T(8,128)S(1)}, f32[32,104,128]{2,1,0:T(8,128)S(1)}, u32[]{:S(2)}, u32[]{:S(2)}) collective-permute-start(f32[32,104,128]{2,1,0:T(8,128)S(1)} %get-tuple-element.23), channel_id=1, source_target_pairs={{0,1},{1,0},{2,3},{3,2},{4,5},{5,4},{6,7},{7,6},{8,9},{9,8},{10,11... | collective-permute-start | bytes 5111816 | tf_op jit(solution)/shard_map/ppermute | solution.py:485
  65.1 8.4 %collective-permute-start.3 = (f32[112,128]{1,0:T(8,128)S(1)}, f32[112,128]{1,0:T(8,128)S(1)}, u32[]{:S(2)}, u32[]{:S(2)}) collective-permute-start(f32[112,128]{1,0:T(8,128)S(1)} %peer_sum.1.own), channel_id=1, source_target_pairs={{0,24},{8,0},{16,8},{24,16},{1,25},{9,1},{17,9},{25,17},{2,26},{10... | collective-permute-start | bytes 172040 | tf_op jit(solution)/shard_map/ppermute | solution.py:497
  70.3 7.1 %collective-permute-start.2 = (f32[112,128]{1,0:T(8,128)S(1)}, f32[112,128]{1,0:T(8,128)S(1)}, u32[]{:S(2)}, u32[]{:S(2)}) collective-permute-start(f32[112,128]{1,0:T(8,128)S(1)} %peer_sum.1.own), channel_id=1, source_target_pairs={{0,16},{8,24},{16,0},{24,8},{1,17},{9,25},{17,1},{25,9},{2,18},{10... | collective-permute-start | bytes 172040 | tf_op jit(solution)/shard_map/ppermute | solution.py:497
  71.5 6.4 %collective-permute-start.1 = (f32[112,128]{1,0:T(8,128)S(1)}, f32[112,128]{1,0:T(8,128)S(1)}, u32[]{:S(2)}, u32[]{:S(2)}) collective-permute-start(f32[112,128]{1,0:T(8,128)S(1)} %peer_sum.1.own), channel_id=1, source_target_pairs={{0,8},{8,16},{16,24},{24,0},{1,9},{9,17},{17,25},{25,1},{2,10},{10... | collective-permute-start | bytes 172040 | tf_op jit(solution)/shard_map/ppermute | solution.py:497
  105.7 7.5 %collective-permute-start.4 = (f32[32,112,128]{2,1,0:T(8,128)S(1)}, f32[32,112,128]{2,1,0:T(8,128)S(1)}, u32[]{:S(2)}, u32[]{:S(2)}) collective-permute-start(f32[32,112,128]{2,1,0:T(8,128)S(1)} %all_to_all.16.rows), channel_id=1, source_target_pairs={{0,1},{1,0},{2,3},{3,2},{4,5},{5,4},{6,7},{7,6},{8,9},{9,8},{10,11... | collective-permute-start | bytes 5505032 | tf_op jit(solution)/shard_map/ppermute | solution.py:502

commit v7 on v6

--- a/solution.py
+++ b/solution.py
@@ -147,7 +147,8 @@
     projected = jnp.dot(rounded, head[...], preferred_element_type=jnp.float32)
     pack_out[0:SEGS, :] = projected
     for index in range(SEGS):
-        row = jnp.full((1, PROJ), positive[0, index], jnp.int32)
+        other = positive[0, index]
+        row = jnp.full((1, PROJ), ((other >> 4) & 1) * 64 + (other >> 5) * SEGS + (other & (SEGS - 1)), jnp.int32)
         pack_out[SEGS + index : SEGS + index + 1, :] = row.astype(jnp.float32)
     for block in range(C // 128):
         at = PACK_POOLED + block * SEGS
@@ -477,9 +478,9 @@
     f32 = jnp.float32
     peers = ("zl", "yh", "yl", "x")
     swap = [(0, 1), (1, 0)]
-    places = jnp.stack([lax.axis_index(("x", "yh")), lax.axis_index("core")]).astype(jnp.int32)
+    places = jnp.stack([lax.axis_index(("yh", "x")), lax.axis_index("core")]).astype(jnp.int32)
     normed, slope, pack, send = forward(group, positive, segments, conv_weight, gain.reshape(1, C), head)
-    gathered = lax.all_to_all(send, ("x", "yh"), 0, 0)
+    gathered = lax.all_to_all(send, ("yh", "x"), 0, 0)
     pack = jnp.where(places[1] >= 0, pack, 0.0)
     grad, keep, give = weight_gradient(places, gathered, pack, normed, slope)
     received = lax.ppermute(give, "core", swap)

time: 115 us -> 115 us (level)
  no operation moved by 1% of the time
where the time goes in v7:
time: 115 us
  blocking collectives  54.7 us (48%)
  Pallas kernels  24.6 us (21%)
  starting transfers between devices  22.2 us (19%)
  waiting for transfers between devices  11.7 us (10%)
    all_to_all x1, blocking collectives, body(): mine = lax.all_to_all(spread, peers, 0, 0)  27.7 us
    all_to_all x1, blocking collectives, body(): across = lax.all_to_all(paired, peers, 0, 0)  27.1 us
    pallas_call x1, Pallas kernels, forward(): pl.pallas_call(forward_kernel, in_specs=[IN_HBM] * 6, out_specs=[IN_HBM]...  9.31 us
    ppermute x3, starting transfers between devices, body(): lax.ppermute(chunk, 'zh', [(i, (i + d) % STACKS) for i in range(STACKS)])  8.43 us
    all_to_all x1, starting transfers between devices, body(): gathered = lax.all_to_all(send, ('yh', 'x'), 0, 0)  7.48 us
    pallas_call x1, Pallas kernels, weight_gradient(): pl.pallas_call(weight_kernel, in_specs=[IN_SMEM, IN_VMEM, IN_VMEM, IN_HBM...  7.48 us
    all_to_all x1, waiting for transfers between devices, body(): gathered = lax.all_to_all(send, ('yh', 'x'), 0, 0)  5.75 us
    ppermute x3, waiting for transfers between devices, body(): lax.ppermute(chunk, 'zh', [(i, (i + d) % STACKS) for i in range(STACKS)])  4.28 us
  transfers between devices with their start and end apart: 6, of which 4 were waited for; matrix products, arithmetic and copies ran while one was open for 1% of the time, Pallas kernels for 5%

profile of v7, /device:TPU:1, one launch (start us, length us, event | category | flops | bytes accessed | tf_op | source)
XLA Modules:
  0.0 114.9 jit_solution(5755211141867531989)
XLA Ops:
  0.6 9.3 %forward.1 = (bf16[16,128,512]{2,1,0:T(8,128)(2,1)}, f32[16,128,512]{2,1,0:T(8,128)}, f32[608,128]{1,0:T(8,128)}, f32[8,24,128]{2,1,0:T(8,128)}) custom-call(s32[1,16]{1,0:T(1,128)} %group_hbm.1, s32[1,16]{1,0:T(1,128)} %positive_hbm.1, bf16[1,16,128,512]{3,2,1,0:T(8,128)(2,1)} %segments.1, bf16[1536,512]{1,0:T(8,128)(2,1)} %bitcast.7, f32[1,512]{1,0:T(1,128)} %bitcast.10, ...), custom_call_target="tpu_custom_call" | custom-call | flops 3221225472 | bytes 10485760 | tf_op jit(solution)/shard_map/forward/pallas_call | solution.py:178
  10.0 7.5 %all-to-all-start = ((f32[8,24,128]{2,1,0:T(8,128)}), f32[8,24,128]{2,1,0:T(8,128)S(1)}, u32[]{:S(2)}, u32[]{:S(2)}) async-start(f32[8,24,128]{2,1,0:T(8,128)} %get-tuple-element.18), calls=%async_computation | async-start | bytes 196608 | tf_op jit(solution)/shard_map/all_to_all | solution.py:483
  17.4 1.0 broadcast_select_fusion.pack
  18.4 0.1 pad_add_fusion.places
  18.5 5.8 %all-to-all-done.gathered = f32[8,24,128]{2,1,0:T(8,128)S(1)} async-done(((f32[8,24,128]{2,1,0:T(8,128)}), f32[8,24,128]{2,1,0:T(8,128)S(1)}, u32[]{:S(2)}, u32[]{:S(2)}) %all-to-all-start) | async-done | bytes 98336 | tf_op jit(solution)/shard_map/all_to_all | solution.py:483
  24.3 0.0 copy-start
  24.3 0.0 copy-start.1
  24.3 7.5 %weight_gradient.1 = (bf16[16,128,512]{2,1,0:T(8,128)(2,1)S(1)}, f32[32,104,128]{2,1,0:T(8,128)S(1)}, f32[32,104,128]{2,1,0:T(8,128)S(1)}) custom-call(s32[2]{0:T(128)S(1)} %pad_add_fusion.places, f32[8,24,128]{2,1,0:T(8,128)S(1)} %all-to-all-done.gathered, f32[608,128]{1,0:T(8,128)S(1)} %broadcast_select_fusion.pack, ...), custom_call_target="tpu_custom_call" | custom-call | flops 3221225472 | bytes 12582912 | tf_op jit(solution)/shard_map/weight_gradient/pallas_call | solution.py:324
  31.8 2.1 %collective-permute-start = (f32[32,104,128]{2,1,0:T(8,128)S(1)}, f32[32,104,128]{2,1,0:T(8,128)S(1)}, u32[]{:S(2)}, u32[]{:S(2)}) collective-permute-start(f32[32,104,128]{2,1,0:T(8,128)S(1)} %get-tuple-element.23), channel_id=1, source_target_pairs={{0,1},{1,0},{2,3},{3,2},{4,5},{5,4},{6,7},{7,6},{8,9},{9,8},{10,11... | collective-permute-start | bytes 5111816 | tf_op jit(solution)/shard_map/ppermute | solution.py:486
  33.9 0.0 copy-done
  33.9 0.0 copy-done.1
  33.9 3.9 %gain_gradient.1.gain = f32[8,128]{1,0:T(8,128)S(1)} custom-call(bf16[16,128,512]{2,1,0:T(8,128)(2,1)S(1)} %get-tuple-element.24.grad, bf16[1,16,128,512]{3,2,1,0:T(8,128)(2,1)S(1)} %copy-done, bf16[3,512,512]{2,1,0:T(8,128)(2,1)S(1)} %copy-done.1), custom_call_target="tpu_custom_call" | custom-call | flops 3221225472 | bytes 6291456 | tf_op jit(solution)/shard_map/gain_gradient/pallas_call | solution.py:381
  37.8 0.0 collective-permute-done.received
  37.8 0.2 pair_sum.1
  38.0 27.1 %all_to_all.15.received = f32[32,104,128]{2,1,0:T(8,128)S(1)} all-to-all(f32[32,104,128]{2,1,0:T(8,128)S(1)} %get-tuple-element.25), channel_id=1, replica_groups=mesh['x'=4,'yh'=2,'zh'=4,'zl'=2,'yl'=2,'core'=2] {'zl','yh','yl','x'}, dimensions={0} | all-to-all | bytes 3407872 | tf_op jit(solution)/shard_map/all_to_all | solution.py:496
  65.0 0.1 peer_sum.1.own
  65.1 5.2 %collective-permute-start.3 = (f32[112,128]{1,0:T(8,128)S(1)}, f32[112,128]{1,0:T(8,128)S(1)}, u32[]{:S(2)}, u32[]{:S(2)}) collective-permute-start(f32[112,128]{1,0:T(8,128)S(1)} %peer_sum.1.own), channel_id=1, source_target_pairs={{0,24},{8,0},{16,8},{24,16},{1,25},{9,1},{17,9},{25,17},{2,26},{10... | collective-permute-start | bytes 172040 | tf_op jit(solution)/shard_map/ppermute | solution.py:498
  70.3 1.2 %collective-permute-start.2 = (f32[112,128]{1,0:T(8,128)S(1)}, f32[112,128]{1,0:T(8,128)S(1)}, u32[]{:S(2)}, u32[]{:S(2)}) collective-permute-start(f32[112,128]{1,0:T(8,128)S(1)} %peer_sum.1.own), channel_id=1, source_target_pairs={{0,16},{8,24},{16,0},{24,8},{1,17},{9,25},{17,1},{25,9},{2,18},{10... | collective-permute-start | bytes 172040 | tf_op jit(solution)/shard_map/ppermute | solution.py:498
  71.5 2.1 %collective-permute-start.1 = (f32[112,128]{1,0:T(8,128)S(1)}, f32[112,128]{1,0:T(8,128)S(1)}, u32[]{:S(2)}, u32[]{:S(2)}) collective-permute-start(f32[112,128]{1,0:T(8,128)S(1)} %peer_sum.1.own), channel_id=1, source_target_pairs={{0,8},{8,16},{16,24},{24,0},{1,9},{9,17},{17,25},{25,1},{2,10},{10... | collective-permute-start | bytes 172040 | tf_op jit(solution)/shard_map/ppermute | solution.py:498
  73.6 0.0 collective-permute-done.3.before
  73.6 3.9 %collective-permute-done.2.across = f32[112,128]{1,0:T(8,128)S(1)} collective-permute-done((f32[112,128]{1,0:T(8,128)S(1)}, f32[112,128]{1,0:T(8,128)S(1)}, u32[]{:S(2)}, u32[]{:S(2)}) %collective-permute-start.2) | collective-permute-done | bytes 57376 | tf_op jit(solution)/shard_map/ppermute | solution.py:498
  77.4 0.4 collective-permute-done.1.after
  77.8 0.1 stack_sum.1
  78.0 27.7 %all_to_all.16.rows = f32[32,112,128]{2,1,0:T(8,128)S(1)} all-to-all(f32[32,112,128]{2,1,0:T(8,128)S(1)} %stack_sum.1), channel_id=1, replica_groups=mesh['x'=4,'yh'=2,'zh'=4,'zl'=2,'yl'=2,'core'=2] {'zl','yh','yl','x'}, dimensions={0} | all-to-all | bytes 3670016 | tf_op jit(solution)/shard_map/all_to_all | solution.py:502
  105.6 4.1 %collective-permute-start.4 = (f32[32,112,128]{2,1,0:T(8,128)S(1)}, f32[32,112,128]{2,1,0:T(8,128)S(1)}, u32[]{:S(2)}, u32[]{:S(2)}) collective-permute-start(f32[32,112,128]{2,1,0:T(8,128)S(1)} %all_to_all.16.rows), channel_id=1, source_target_pairs={{0,1},{1,0},{2,3},{3,2},{4,5},{5,4},{6,7},{7,6},{8,9},{9,8},{10,11... | collective-permute-start | bytes 5505032 | tf_op jit(solution)/shard_map/ppermute | solution.py:503
  109.7 1.8 %place_mine.1 = (f32[3,32,16,512]{3,2,1,0:T(8,128)}, f32[2,32,8,128]{3,2,1,0:T(8,128)}, f32[8,128]{1,0:T(8,128)S(1)}) custom-call(s32[2]{0:T(128)S(1)} %pad_add_fusion.places, f32[32,112,128]{2,1,0:T(8,128)S(1)} %all_to_all.16.rows), custom_call_target="tpu_custom_call" | custom-call | flops 1048576 | bytes 4194304 | tf_op jit(solution)/shard_map/place_mine/pallas_call | solution.py:460
  111.5 1.6 %collective-permute-done.4.rows = f32[32,112,128]{2,1,0:T(8,128)S(1)} collective-permute-done((f32[32,112,128]{2,1,0:T(8,128)S(1)}, f32[32,112,128]{2,1,0:T(8,128)S(1)}, u32[]{:S(2)}, u32[]{:S(2)}) %collective-permute-start.4) | collective-permute-done | bytes 1835040 | tf_op jit(solution)/shard_map/ppermute | solution.py:503
  113.2 1.8 %place_other.1 = (f32[3,32,16,512]{3,2,1,0:T(8,128)}, f32[2,32,8,128]{3,2,1,0:T(8,128)}, f32[4,128]{1,0:T(4,128)}) custom-call(s32[2]{0:T(128)S(1)} %pad_add_fusion.places, f32[32,112,128]{2,1,0:T(8,128)S(1)} %collective-permute-done.4.rows, f32[8,128]{1,0:T(8,128)S(1)} %get-tuple-element.27.refs_0_, ...), custom_call_target="tpu_custom_call", output_to_operand_aliasing={{0}: (3, {}), {1}: (4, {})} | custom-call | flops 1048576 | bytes 4194304 | tf_op jit(solution)/shard_map/place_other/pallas_call | solution.py:460
Async XLA Ops:
  10.0 14.3 %all-to-all-start = ((f32[8,24,128]{2,1,0:T(8,128)}), f32[8,24,128]{2,1,0:T(8,128)S(1)}, u32[]{:S(2)}, u32[]{:S(2)}) async-start(f32[8,24,128]{2,1,0:T(8,128)} %get-tuple-element.18), calls=%async_computation | async-start | bytes 196608 | tf_op jit(solution)/shard_map/all_to_all | solution.py:483
  24.3 9.6 %copy-start = (bf16[1,16,128,512]{3,2,1,0:T(8,128)(2,1)S(1)}, bf16[1,16,128,512]{3,2,1,0:T(8,128)(2,1)}, u32[]{:S(2)}) copy-start(bf16[1,16,128,512]{3,2,1,0:T(8,128)(2,1)} %segments.1) | copy-start | bytes 6291460
  24.3 9.6 %copy-start.1 = (bf16[3,512,512]{2,1,0:T(8,128)(2,1)S(1)}, bf16[3,512,512]{2,1,0:T(8,128)(2,1)}, u32[]{:S(2)}) copy-start(bf16[3,512,512]{2,1,0:T(8,128)(2,1)} %weight.1) | copy-start | bytes 4718596
  31.8 6.0 %collective-permute-start = (f32[32,104,128]{2,1,0:T(8,128)S(1)}, f32[32,104,128]{2,1,0:T(8,128)S(1)}, u32[]{:S(2)}, u32[]{:S(2)}) collective-permute-start(f32[32,104,128]{2,1,0:T(8,128)S(1)} %get-tuple-element.23), channel_id=1, source_target_pairs={{0,1},{1,0},{2,3},{3,2},{4,5},{5,4},{6,7},{7,6},{8,9},{9,8},{10,11... | collective-permute-start | bytes 5111816 | tf_op jit(solution)/shard_map/ppermute | solution.py:486
  65.1 8.4 %collective-permute-start.3 = (f32[112,128]{1,0:T(8,128)S(1)}, f32[112,128]{1,0:T(8,128)S(1)}, u32[]{:S(2)}, u32[]{:S(2)}) collective-permute-start(f32[112,128]{1,0:T(8,128)S(1)} %peer_sum.1.own), channel_id=1, source_target_pairs={{0,24},{8,0},{16,8},{24,16},{1,25},{9,1},{17,9},{25,17},{2,26},{10... | collective-permute-start | bytes 172040 | tf_op jit(solution)/shard_map/ppermute | solution.py:498
  70.3 7.1 %collective-permute-start.2 = (f32[112,128]{1,0:T(8,128)S(1)}, f32[112,128]{1,0:T(8,128)S(1)}, u32[]{:S(2)}, u32[]{:S(2)}) collective-permute-start(f32[112,128]{1,0:T(8,128)S(1)} %peer_sum.1.own), channel_id=1, source_target_pairs={{0,16},{8,24},{16,0},{24,8},{1,17},{9,25},{17,1},{25,9},{2,18},{10... | collective-permute-start | bytes 172040 | tf_op jit(solution)/shard_map/ppermute | solution.py:498
  71.5 6.4 %collective-permute-start.1 = (f32[112,128]{1,0:T(8,128)S(1)}, f32[112,128]{1,0:T(8,128)S(1)}, u32[]{:S(2)}, u32[]{:S(2)}) collective-permute-start(f32[112,128]{1,0:T(8,128)S(1)} %peer_sum.1.own), channel_id=1, source_target_pairs={{0,8},{8,16},{16,24},{24,0},{1,9},{9,17},{17,25},{25,1},{2,10},{10... | collective-permute-start | bytes 172040 | tf_op jit(solution)/shard_map/ppermute | solution.py:498
  105.6 7.5 %collective-permute-start.4 = (f32[32,112,128]{2,1,0:T(8,128)S(1)}, f32[32,112,128]{2,1,0:T(8,128)S(1)}, u32[]{:S(2)}, u32[]{:S(2)}) collective-permute-start(f32[32,112,128]{2,1,0:T(8,128)S(1)} %all_to_all.16.rows), channel_id=1, source_target_pairs={{0,1},{1,0},{2,3},{3,2},{4,5},{5,4},{6,7},{7,6},{8,9},{9,8},{10,11... | collective-permute-start | bytes 5505032 | tf_op jit(solution)/shard_map/ppermute | solution.py:503
